TPU v7x, 32 devices: a whole 2x2x4 slice. The times are simulated.
32 devices in a mesh: win: 4 (over y, x), seq: 8 (over z, core).
Axes of the slice: x: 2, y: 2, z: 4, core: 2. Of those that a mesh axis runs over, the one named last changes fastest.
Arguments:
- tokens: bfloat16 [8, 1024, 768], P('win', 'seq'), may hold values from -6 to 6
- cotangent: bfloat16 [8, 1024, 768], P('win', 'seq'), may hold values from -6 to 6
- group_ids: int32 [8], P('win'), may hold values from 0 to 7
- random_blocks: int32 [8, 16, 3], P('win'), may hold values from 0 to 15, as said below
- norm1_gain: float32 [768], replicated, may hold values from 0.25 to 1.75
- norm1_bias: float32 [768], replicated, may hold values from -1.25 to 1.25
- query_weight: bfloat16 [768, 768], replicated, may hold values from -0.21875 to 0.21875
- query_bias: float32 [768], replicated, may hold values from -1.25 to 1.25
- key_weight: bfloat16 [768, 768], replicated, may hold values from -0.21875 to 0.21875
- value_weight: bfloat16 [768, 768], replicated, may hold values from -0.21875 to 0.21875
- value_bias: float32 [768], replicated, may hold values from -1.25 to 1.25
- out_weight: bfloat16 [768, 768], replicated, may hold values from -1.75 to 1.75
- out_bias: float32 [768], replicated, may hold values from -1.25 to 1.25
- norm2_gain: float32 [768], replicated, may hold values from 0.25 to 1.75
- norm2_bias: float32 [768], replicated, may hold values from -1.25 to 1.25
- up_weight: bfloat16 [768, 3072], replicated, may hold values from -0.21875 to 0.21875
- up_bias: float32 [3072], replicated, may hold values from -1.25 to 1.25
- down_weight: bfloat16 [3072, 768], replicated, may hold values from -0.109375 to 0.109375
- down_bias: float32 [768], replicated, may hold values from -1.25 to 1.25
Outputs:
- output: bfloat16 [8, 1024, 768], P('win', 'seq')
- input_grad: bfloat16 [8, 1024, 768], P('win', 'seq')
- norm1_gain_grad: float32 [768], replicated
- norm1_bias_grad: float32 [768], replicated
- query_weight_grad: float32 [768, 768], replicated
- query_bias_grad: float32 [768], replicated
- key_weight_grad: float32 [768, 768], replicated
- value_weight_grad: float32 [768, 768], replicated
- value_bias_grad: float32 [768], replicated
- out_weight_grad: float32 [768, 768], replicated
- out_bias_grad: float32 [768], replicated
- norm2_gain_grad: float32 [768], replicated
- norm2_bias_grad: float32 [768], replicated
- up_weight_grad: float32 [768, 3072], replicated
- up_bias_grad: float32 [3072], replicated
- down_weight_grad: float32 [3072, 768], replicated
- down_bias_grad: float32 [768], replicated
Inputs may be any that keep to these rules, and one draw needn't show every extreme that they name: `random_blocks`: take the windows in aligned groups of 1 (one micro-batch of one index of win) and the blocks in aligned runs of 2 (block b lies in run b // 2). Within one group of windows, the 6 random entries of the query blocks of one run name blocks of any one run at most 1 times, and in every group some run names blocks of one run exactly 1 times.
All inputs are finite; a program needn't handle non-finite values.
Results may differ from a plain program's by a relative error of at most 0.014.
Values may be sent and summed in bfloat16 or wider, within the bound.
A program may use at most 256 MiB of HBM per device.

v0:
```python
import jax
import jax.numpy as jnp
from jax import lax
from jax.sharding import PartitionSpec as P

D = 768
HEADS = 12
HEAD_DIM = 64
BLOCK = 64
RAND = 3
BLK_DEV = 2
MICRO = 2
WIN_MB = 1
GROUPS = 8


epsilon = 1e-05
masked_score = -1e30
highest = lax.Precision.HIGHEST


def with_halo(block, sides, width):
    for axis, dim in sides:
        count = lax.axis_size(axis)
        forward = [(i, i + 1) for i in range(count - 1)]
        backward = [(target, source) for source, target in forward]
        low = lax.ppermute(
            lax.slice_in_dim(block, block.shape[dim] - width, None, axis=dim), axis, forward
        )
        high = lax.ppermute(lax.slice_in_dim(block, 0, width, axis=dim), axis, backward)
        block = jnp.concatenate([low, block, high], axis=dim)
    return block


def from_root(x, axis, root):
    mine = lax.axis_index(axis) == root
    return lax.psum(jnp.where(mine, x, jnp.zeros_like(x)), axis)


def layer_norm(inputs, gain_row, shift_row):
    centre = inputs - jnp.mean(inputs, axis=-1, keepdims=True)
    spread = jnp.mean(centre * centre, axis=-1, keepdims=True)
    return centre * lax.rsqrt(spread + epsilon) * gain_row + shift_row


def activate(inputs):
    return jax.nn.gelu(inputs, approximate=False)


def project(inputs, weights):
    return jnp.einsum("wld,de->wle", inputs, weights, preferred_element_type=jnp.float32)


def project_back(gradient, weights):
    return jnp.einsum("wle,de->wld", gradient, weights, preferred_element_type=jnp.float32)


def weight_grad(inputs, gradient):
    return jnp.einsum("wld,wle->de", inputs, gradient, preferred_element_type=jnp.float32)


def column_sum(gradient):
    return jnp.sum(gradient.astype(jnp.float32), axis=(0, 1))


def route_tables(chosen_blocks, seq_count, places, seq_index):
    windows_here = chosen_blocks.shape[0]
    picks_each = chosen_blocks.shape[2]
    per_peer = chosen_blocks.reshape(windows_here, seq_count, BLK_DEV, picks_each)
    per_peer = jnp.transpose(per_peer, (1, 0, 2, 3)).reshape(
        seq_count, windows_here * BLK_DEV * picks_each
    )
    owner_of = per_peer // BLK_DEV
    request_ids = jnp.arange(per_peer.shape[1])
    earlier = request_ids[None, :] < request_ids[:, None]
    same_owner = owner_of[:, :, None] == owner_of[:, None, :]
    rank_in = jnp.sum(jnp.where(same_owner & earlier[None, :, :], 1, 0), axis=2)
    home_block = request_ids[None, :] // (BLK_DEV * picks_each) * BLK_DEV + per_peer % BLK_DEV
    slot_ids = jnp.arange(places)
    block_ids = jnp.arange(windows_here * BLK_DEV)
    for_me = (owner_of == seq_index)[:, :, None, None]
    slot_match = (rank_in[:, :, None] == slot_ids[None, None, :])[:, :, :, None]
    block_match = (home_block[:, :, None] == block_ids[None, None, :])[:, :, None, :]
    send_pick = jnp.any(for_me & slot_match & block_match, axis=1)
    my_owner = lax.dynamic_index_in_dim(owner_of, seq_index, 0, keepdims=False)
    my_rank = lax.dynamic_index_in_dim(rank_in, seq_index, 0, keepdims=False)
    peer_ids = jnp.arange(seq_count)
    recv_pick = (my_owner[:, None, None] == peer_ids[None, :, None]) & (
        my_rank[:, None, None] == slot_ids[None, None, :]
    )
    return (send_pick, recv_pick)


def key_usable(seq_index, seq_count):
    block_ids = jnp.arange(BLK_DEV)
    left_ok = (seq_index > 0) | (block_ids > 0)
    right_ok = (seq_index < seq_count - 1) | (block_ids < BLK_DEV - 1)
    always = jnp.ones((BLK_DEV,), dtype=bool)
    usable = jnp.stack([left_ok, always, right_ok, always, always] + [always] * RAND, axis=1)
    return jnp.repeat(usable, BLOCK, axis=1)


def build_context(key_value, send_pick, recv_pick, seq_count):
    windows_here, row_count, channels = key_value.shape
    padded = with_halo(key_value, (("seq", 1),), BLOCK)
    first_keys = from_root(key_value[:, :BLOCK], "seq", 0)
    last_keys = from_root(key_value[:, row_count - BLOCK :], "seq", seq_count - 1)
    blocks_here = key_value.reshape(windows_here * BLK_DEV, BLOCK * channels)
    outgoing = jnp.einsum(
        "pcl,lf->pcf",
        send_pick.astype(jnp.bfloat16),
        blocks_here,
        preferred_element_type=jnp.float32,
    ).astype(jnp.bfloat16)
    arrived = lax.all_to_all(outgoing, "seq", split_axis=0, concat_axis=0, tiled=True)
    fetched = jnp.einsum(
        "esc,scf->ef", recv_pick.astype(jnp.bfloat16), arrived, preferred_element_type=jnp.float32
    ).astype(jnp.bfloat16)
    stacked = padded.reshape(windows_here, BLK_DEV + 2, BLOCK, channels)
    sliding = jnp.stack(
        [stacked[:, 0:BLK_DEV], stacked[:, 1 : BLK_DEV + 1], stacked[:, 2 : BLK_DEV + 2]], axis=2
    )
    global_pair = jnp.stack([first_keys, last_keys], axis=1)[:, None]
    global_pair = jnp.broadcast_to(global_pair, (windows_here, BLK_DEV, 2, BLOCK, channels))
    random_part = fetched.reshape(windows_here, BLK_DEV, RAND, BLOCK, channels)
    return jnp.concatenate([sliding, global_pair, random_part], axis=2)


def spread_context_grad(context_grad, send_pick, recv_pick, seq_index, seq_count):
    windows_here = context_grad.shape[0]
    channels = context_grad.shape[-1]
    spread = (
        jnp.pad(context_grad[:, :, 0], ((0, 0), (0, 2), (0, 0), (0, 0)))
        + jnp.pad(context_grad[:, :, 1], ((0, 0), (1, 1), (0, 0), (0, 0)))
        + jnp.pad(context_grad[:, :, 2], ((0, 0), (2, 0), (0, 0), (0, 0)))
    )
    own_part = spread[:, 1 : BLK_DEV + 1].reshape(windows_here, BLK_DEV * BLOCK, channels)
    rim_grads = jnp.concatenate([spread[:, 0], spread[:, BLK_DEV + 1]], axis=1)
    returned = with_halo(rim_grads.astype(jnp.bfloat16), (("seq", 1),), BLOCK).astype(
        rim_grads.dtype
    )
    from_prev = returned[:, :BLOCK]
    from_next = returned[:, 3 * BLOCK :]
    global_part = jnp.sum(context_grad[:, :, 3:5], axis=1)
    global_total = lax.psum(global_part.astype(jnp.bfloat16), "seq").astype(jnp.float32)
    first_add = jnp.where(seq_index == 0, global_total[:, 0], 0.0)
    last_add = jnp.where(seq_index == seq_count - 1, global_total[:, 1], 0.0)
    random_part = context_grad[:, :, 5:].reshape(-1, BLOCK * channels)
    going_back = jnp.einsum(
        "esc,ef->scf", recv_pick.astype(jnp.float32), random_part, precision=highest
    )
    came_back = lax.all_to_all(
        going_back.astype(jnp.bfloat16), "seq", split_axis=0, concat_axis=0, tiled=True
    ).astype(going_back.dtype)
    random_home = jnp.einsum(
        "pcl,pcf->lf", send_pick.astype(jnp.float32), came_back, precision=highest
    )
    random_home = random_home.reshape(windows_here, BLK_DEV * BLOCK, channels)
    middle = jnp.zeros((windows_here, (BLK_DEV - 2) * BLOCK, channels), jnp.float32)
    edge_grads = jnp.concatenate([from_prev + first_add, middle, from_next + last_add], axis=1)
    return own_part + edge_grads + random_home


def body(
    tokens,
    cotangent,
    group_ids,
    random_blocks,
    norm1_gain,
    norm1_bias,
    query_weight,
    query_bias,
    key_weight,
    value_weight,
    value_bias,
    out_weight,
    out_bias,
    norm2_gain,
    norm2_bias,
    up_weight,
    up_bias,
    down_weight,
    down_bias,
):
    seq_count = lax.axis_size("seq")
    seq_index = lax.axis_index("seq")
    score_scale = HEAD_DIM ** (-0.5)
    key_slots = 5 + RAND
    slots_each = WIN_MB * BLK_DEV * RAND // seq_count + 1
    membership = (group_ids[:, None] == jnp.arange(GROUPS)[None, :]).astype(jnp.float32)
    group_sizes = lax.psum(jnp.sum(membership, axis=0), "win")
    window_total = group_ids.shape[0] * lax.axis_size("win")
    window_scale = window_total / (GROUPS * jnp.sum(membership * group_sizes[None, :], axis=1))
    usable = key_usable(seq_index, seq_count)[None, :, None, None, :]
    totals = None
    output_rows = []
    input_grads = []
    for micro_index in range(MICRO):
        first_row = micro_index * WIN_MB
        inputs = tokens[first_row : first_row + WIN_MB].astype(jnp.float32)
        send_pick, recv_pick = route_tables(
            random_blocks[first_row : first_row + WIN_MB], seq_count, slots_each, seq_index
        )
        normed, norm1_pull = jax.vjp(layer_norm, inputs, norm1_gain, norm1_bias)
        normed_low = normed.astype(jnp.bfloat16)
        queries = (project(normed_low, query_weight) + query_bias).astype(jnp.bfloat16)
        keys_low = project(normed_low, key_weight).astype(jnp.bfloat16)
        values_low = (project(normed_low, value_weight) + value_bias).astype(jnp.bfloat16)
        key_value = jnp.concatenate([keys_low, values_low], axis=-1)
        context = build_context(key_value, send_pick, recv_pick, seq_count)
        query_heads = queries.reshape(WIN_MB, BLK_DEV, BLOCK, HEADS, HEAD_DIM)
        context_keys = context[..., :D].reshape(WIN_MB, BLK_DEV, key_slots * BLOCK, HEADS, HEAD_DIM)
        context_values = context[..., D:].reshape(
            WIN_MB, BLK_DEV, key_slots * BLOCK, HEADS, HEAD_DIM
        )
        scores = (
            jnp.einsum(
                "wbqhd,wbkhd->wbhqk", query_heads, context_keys, preferred_element_type=jnp.float32
            )
            * score_scale
        )
        scores = jnp.where(usable, scores, masked_score)
        row_top = jnp.max(scores, axis=-1, keepdims=True)
        exponent = jnp.exp(scores - row_top)
        row_mass = jnp.sum(exponent, axis=-1, keepdims=True)
        log_mass = row_top + jnp.log(row_mass)
        softmax_low = (exponent / row_mass).astype(jnp.bfloat16)
        attended = jnp.einsum(
            "wbhqk,wbkhd->wbqhd", softmax_low, context_values, preferred_element_type=jnp.float32
        )
        attended_low = attended.reshape(WIN_MB, BLK_DEV * BLOCK, D).astype(jnp.bfloat16)
        hidden = inputs + (project(attended_low, out_weight) + out_bias)
        normed_two, norm2_pull = jax.vjp(layer_norm, hidden, norm2_gain, norm2_bias)
        normed_two_low = normed_two.astype(jnp.bfloat16)
        pre_act = project(normed_two_low, up_weight) + up_bias
        activated, act_pull = jax.vjp(activate, pre_act)
        act_low = activated.astype(jnp.bfloat16)
        outputs = hidden + project(act_low, down_weight) + down_bias
        output_rows.append(outputs.astype(jnp.bfloat16))
        out_grad = (
            cotangent[first_row : first_row + WIN_MB].astype(jnp.float32)
            * window_scale[first_row : first_row + WIN_MB, None, None]
        ).astype(jnp.bfloat16)
        down_grad = weight_grad(act_low, out_grad)
        down_bias_grad = column_sum(out_grad)
        pre_grad = act_pull(project_back(out_grad, down_weight))[0].astype(jnp.bfloat16)
        up_grad = weight_grad(normed_two_low, pre_grad)
        up_bias_grad = column_sum(pre_grad)
        hidden_grad, norm2_gain_grad, norm2_bias_grad = norm2_pull(
            project_back(pre_grad, up_weight)
        )
        hidden_grad = hidden_grad + out_grad.astype(jnp.float32)
        branch_grad = hidden_grad.astype(jnp.bfloat16)
        out_weight_grad = weight_grad(attended_low, branch_grad)
        out_bias_grad = column_sum(branch_grad)
        attended_grad = project_back(branch_grad, out_weight).astype(jnp.bfloat16)
        grad_heads = attended_grad.reshape(WIN_MB, BLK_DEV, BLOCK, HEADS, HEAD_DIM)
        scores_again = (
            jnp.einsum(
                "wbqhd,wbkhd->wbhqk", query_heads, context_keys, preferred_element_type=jnp.float32
            )
            * score_scale
        )
        scores_again = jnp.where(usable, scores_again, masked_score)
        softmax_again = jnp.exp(scores_again - log_mass)
        softmax_again_low = softmax_again.astype(jnp.bfloat16)
        prob_grad = jnp.einsum(
            "wbqhd,wbkhd->wbhqk", grad_heads, context_values, preferred_element_type=jnp.float32
        )
        row_dot = jnp.sum(softmax_again * prob_grad, axis=-1, keepdims=True)
        score_grad = (softmax_again * (prob_grad - row_dot)).astype(jnp.bfloat16)
        query_grad = (
            (
                jnp.einsum(
                    "wbhqk,wbkhd->wbqhd",
                    score_grad,
                    context_keys,
                    preferred_element_type=jnp.float32,
                )
                * score_scale
            )
            .astype(jnp.bfloat16)
            .reshape(WIN_MB, BLK_DEV * BLOCK, D)
        )
        key_grad = (
            jnp.einsum(
                "wbhqk,wbqhd->wbkhd", score_grad, query_heads, preferred_element_type=jnp.float32
            )
            * score_scale
        )
        value_grad = jnp.einsum(
            "wbhqk,wbqhd->wbkhd", softmax_again_low, grad_heads, preferred_element_type=jnp.float32
        )
        context_grad = jnp.concatenate(
            [
                key_grad.reshape(WIN_MB, BLK_DEV, key_slots, BLOCK, D),
                value_grad.reshape(WIN_MB, BLK_DEV, key_slots, BLOCK, D),
            ],
            axis=-1,
        )
        key_value_grad = spread_context_grad(
            context_grad, send_pick, recv_pick, seq_index, seq_count
        ).astype(jnp.bfloat16)
        key_grad_low = key_value_grad[..., :D]
        value_grad_low = key_value_grad[..., D:]
        query_weight_grad = weight_grad(normed_low, query_grad)
        query_bias_grad = column_sum(query_grad)
        key_weight_grad = weight_grad(normed_low, key_grad_low)
        value_weight_grad = weight_grad(normed_low, value_grad_low)
        value_bias_grad = column_sum(value_grad_low)
        normed_grad = (
            project_back(query_grad, query_weight)
            + project_back(key_grad_low, key_weight)
            + project_back(value_grad_low, value_weight)
        )
        input_part, norm1_gain_grad, norm1_bias_grad = norm1_pull(normed_grad)
        input_grads.append((hidden_grad + input_part).astype(jnp.bfloat16))
        pieces = (
            norm1_gain_grad,
            norm1_bias_grad,
            query_weight_grad,
            query_bias_grad,
            key_weight_grad,
            value_weight_grad,
            value_bias_grad,
            out_weight_grad,
            out_bias_grad,
            norm2_gain_grad,
            norm2_bias_grad,
            up_grad,
            up_bias_grad,
            down_grad,
            down_bias_grad,
        )
        if totals is None:
            totals = tuple(pieces)
        else:
            totals = tuple((running_sum + latest for running_sum, latest in zip(totals, pieces)))
    (
        gain1_total,
        shift1_total,
        query_total,
        query_bias_total,
        key_total,
        value_total,
        value_bias_total,
        out_total,
        out_bias_total,
        gain2_total,
        shift2_total,
        up_total,
        up_bias_total,
        down_total,
        down_bias_total,
    ) = totals
    summed = lax.psum(
        (
            gain1_total,
            shift1_total,
            query_total,
            query_bias_total,
            key_total,
            value_total,
            value_bias_total,
            out_total,
            out_bias_total,
            gain2_total,
            shift2_total,
            up_total,
            up_bias_total,
            down_total,
            down_bias_total,
        ),
        ("win", "seq"),
    )
    return (jnp.concatenate(output_rows, axis=0), jnp.concatenate(input_grads, axis=0)) + tuple(
        summed
    )


def solution(mesh):
    placed = (
        P("win", "seq", None),
        P("win", "seq", None),
        P("win"),
        P("win", None, None),
        P(),
        P(),
        P(),
        P(),
        P(),
        P(),
        P(),
        P(),
        P(),
        P(),
        P(),
        P(),
        P(),
        P(),
        P(),
    )
    return jax.shard_map(
        body,
        mesh=mesh,
        in_specs=placed,
        out_specs=(
            P("win", "seq", None),
            P("win", "seq", None),
            P(),
            P(),
            P(),
            P(),
            P(),
            P(),
            P(),
            P(),
            P(),
            P(),
            P(),
            P(),
            P(),
            P(),
            P(),
        ),
        check_vma=False,
    )
```

profile of v0, /device:TPU:0, one launch (start us, length us, event | category | flops | bytes accessed | tf_op | source)
XLA Modules:
  0.0 1073.3 jit_solution(15051027906253139627)
XLA Ops:
  26.0 6.3 all-to-all-start
  47.6 10.6 psum.158
  78.6 6.0 all-to-all-start.1
  149.9 6.3 reshape.1795
  166.3 29.8 %concatenate.139 = bf16[1,2,8,64,1536]{3,2,4,1,0:T(8,128)(2,1)} concatenate(bf16[1,2,1,64,1536]{3,2,4,1,0:T(2,128)(2,1)} %copy.329, bf16[1,2,1,64,1536]{3,2,4,1,0:T(2,128)(2,1)} %copy.330, bf16[1,2,1,64,1536]{3,2,4,1,0:T(2,128)(2,1)} %copy.331, bf16[1,2,2,64,1536]{3,2,4,1,0:T(2,128)(2,1)S(1)} %broadcast_in_dim.78, bf16[1,2,3,64,1536]{3,2,4,1,0:T(4,128)(2,1)} %copy.332), dimensions={2} | concatenate | bytes 6291456 | tf_op jit(solution)/shard_map/concatenate | solution.py:126
  196.1 5.9 fusion.194
  202.0 5.4 reshape.1760
  207.4 5.5 reshape.1758
  219.0 30.0 %concatenate.136 = bf16[1,2,8,64,1536]{3,2,4,1,0:T(8,128)(2,1)} concatenate(bf16[1,2,1,64,1536]{3,2,4,1,0:T(2,128)(2,1)} %copy.312, bf16[1,2,1,64,1536]{3,2,4,1,0:T(2,128)(2,1)} %copy.313, bf16[1,2,1,64,1536]{3,2,4,1,0:T(2,128)(2,1)} %copy.314, bf16[1,2,2,64,1536]{3,2,4,1,0:T(2,128)(2,1)S(1)} %broadcast_in_dim.70, bf16[1,2,3,64,1536]{3,2,4,1,0:T(4,128)(2,1)} %copy.315), dimensions={2} | concatenate | bytes 6291456 | tf_op jit(solution)/shard_map/concatenate | solution.py:126
  249.0 5.9 fusion.193
  259.4 6.0 reshape.1749
  282.0 7.6 multiply_convert_fusion.2
  289.6 5.3 convert_reduce_fusion
  297.2 5.1 multiply_convert_fusion.3
  342.7 5.6 reshape.1766
  348.3 5.8 reshape.1767
  365.7 5.6 reshape.1778
  371.2 5.6 reshape.1779
  400.3 7.7 copy.404
  408.0 5.2 copy.349
  439.1 5.3 copy.361
  447.7 5.9 fusion.121
  478.7 9.6 convolution_add_fusion
  488.3 5.3 convolution_add_fusion.1
  500.4 37.7 %all-reduce.16.cloned.1.call-done = (bf16[1,2,64,1536]{2,1,3,0:T(2,128)(2,1)}, bf16[1,2,64,1536]{2,3,1,0:T(8,128)(2,1)}) async-done(((bf16[1,2,64,1536]{2,1,3,0:T(2,128)(2,1)}, bf16[1,2,64,1536]{2,3,1,0:T(8,128)(2,1)}), (bf16[1,2,64,1536]{2,1,3,0:T(2,128)(2,1)}, bf16[1,2,64,1536]{2,3,1,0:T(8,128)(2,1)})) %all-reduce.16.cloned.1.call-update) | async-done | bytes 786448 | tf_op jit(solution)/shard_map/psum | solution.py:145
  553.9 6.3 reshape.1799
  574.1 11.3 %all-to-all-done.3 = bf16[8,2,49152]{2,1,0:T(2,128)(2,1)} async-done(((bf16[8,2,49152]{2,1,0:T(2,128)(2,1)}), bf16[8,2,49152]{2,1,0:T(2,128)(2,1)}, u32[]{:S(2)}, u32[]{:S(2)}) %all-to-all-start.3) | async-done | bytes 1572896 | tf_op jit(solution)/shard_map/all_to_all | solution.py:152
  585.4 6.6 reshape.1801
  591.9 4.7 fusion.12
  635.2 40.8 %all-reduce.6 = (f32[768]{0:T(1024)}, f32[768]{0:T(1024)}, f32[768]{0:T(1024)}, f32[768]{0:T(1024)}, f32[768]{0:T(1024)}, /*index=5*/f32[768]{0:T(1024)}, f32[768]{0:T(1024)}, f32[3072]{0:T(1024)}, f32[768]{0:T(1024)}) all-reduce(f32[768]{0:T(1024)S(1)} %add.528, f32[768]{0:T(1024)S(1)} %add.529, ...), channel_id=1, replica_groups=mesh['win'=4,'seq'=8] {'win','seq'}, use_global_device_ids=true, to_apply=%region_39.40 | all-reduce | flops 9216 | bytes 73728 | tf_op jit(solution)/shard_map/psum | solution.py:356
  680.0 363.4 %all-reduce.14.cloned.1.call-done = (f32[768,768]{1,0:T(8,128)}, f32[768,768]{1,0:T(8,128)}, f32[768,768]{1,0:T(8,128)}, f32[768,768]{1,0:T(8,128)}, f32[768,3072]{1,0:T(8,128)}, /*index=5*/f32[3072,768]{1,0:T(8,128)}) async-done(((f32[768,768]{1,0:T(8,128)}, f32[768,768]{1,0:T(8,128)}, f32[768,768]{1,0:T(8,128)}, f32[768,768]{1,0:T(8,128)}, f32[768,3072]{1,0:T(8,128)}, /*index=5*/f32[3072,768]{1,0:T(8,128)}), ...) | async-done | bytes 28311568 | tf_op jit(solution)/shard_map/psum | solution.py:356
  1053.2 9.3 copy.427
  (549 shorter events, 380.1 us)
Async XLA Ops:
  17.0 15.3 %copy-start.60 = (bf16[1,128,768]{2,1,0:T(8,128)(2,1)}, bf16[1,128,768]{2,1,0:T(8,128)(2,1)S(1)}, u32[]{:S(2)}) copy-start(bf16[1,128,768]{2,1,0:T(8,128)(2,1)S(1)} %fusion.58) | copy-start | bytes 589828
  17.4 14.9 %copy-start.61 = (bf16[1,128,768]{2,1,0:T(8,128)(2,1)}, bf16[1,128,768]{2,1,0:T(8,128)(2,1)S(1)}, u32[]{:S(2)}) copy-start(bf16[1,128,768]{2,1,0:T(8,128)(2,1)S(1)} %fusion.61) | copy-start | bytes 589828
  26.0 52.6 %all-to-all-start = ((bf16[8,2,49152]{2,1,0:T(2,128)(2,1)}), bf16[8,2,49152]{2,1,0:T(2,128)(2,1)S(1)}, u32[]{:S(2)}, u32[]{:S(2)}) async-start(bf16[8,2,49152]{2,1,0:T(2,128)(2,1)} %reshape.1796), calls=%async_computation | async-start | bytes 3145728 | tf_op jit(solution)/shard_map/all_to_all | solution.py:115
  32.3 99.0 %all-reduce.18.cloned.1.call-start = ((), (), s32[]{:S(2)}) async-start(), calls=%async_computation.6 | async-start | bytes 1572864 | tf_op jit(solution)/shard_map/psum | solution.py:37
  33.4 69.2 %collective-permute-start.1 = (bf16[1,64,1536]{2,1,0:T(8,128)(2,1)}, bf16[1,64,1536]{2,1,0:T(8,128)(2,1)}, u32[]{:S(2)}, u32[]{:S(2)}) collective-permute-start(bf16[1,64,1536]{2,1,0:T(8,128)(2,1)} %get-tuple-element.71), channel_id=1, source_target_pairs={{1,0},{2,1},{3,2},{4,3},{5,4},{6,5},{7,6},{9,8},{10,9},{11,10},{12... | collective-permute-start | bytes 589832 | tf_op jit(solution)/shard_map/ppermute | solution.py:30
  34.6 67.9 %collective-permute-start = (bf16[1,64,1536]{2,1,0:T(8,128)(2,1)}, bf16[1,64,1536]{2,1,0:T(8,128)(2,1)}, u32[]{:S(2)}, u32[]{:S(2)}) collective-permute-start(bf16[1,64,1536]{2,1,0:T(8,128)(2,1)} %get-tuple-element.107), channel_id=1, source_target_pairs={{0,1},{1,2},{2,3},{3,4},{4,5},{5,6},{6,7},{8,9},{9,10},{10,11},{11... | collective-permute-start | bytes 589832 | tf_op jit(solution)/shard_map/ppermute | solution.py:27
  40.7 20.5 %copy-start.62 = (bf16[1,128,768]{2,1,0:T(8,128)(2,1)}, bf16[1,128,768]{2,1,0:T(8,128)(2,1)S(1)}, u32[]{:S(2)}) copy-start(bf16[1,128,768]{2,1,0:T(8,128)(2,1)S(1)} %fusion.59) | copy-start | bytes 589828
  41.1 22.9 %copy-start.63 = (bf16[1,128,768]{2,1,0:T(8,128)(2,1)}, bf16[1,128,768]{2,1,0:T(8,128)(2,1)S(1)}, u32[]{:S(2)}) copy-start(bf16[1,128,768]{2,1,0:T(8,128)(2,1)S(1)} %fusion.60) | copy-start | bytes 589828
  42.1 53.6 %collective-permute-start.2 = (bf16[1,64,1536]{2,1,0:T(8,128)(2,1)}, bf16[1,64,1536]{2,1,0:T(8,128)(2,1)}, u32[]{:S(2)}, u32[]{:S(2)}) collective-permute-start(bf16[1,64,1536]{2,1,0:T(8,128)(2,1)} %get-tuple-element.77), channel_id=1, source_target_pairs={{0,1},{1,2},{2,3},{3,4},{4,5},{5,6},{6,7},{8,9},{9,10},{10,11},{11... | collective-permute-start | bytes 589832 | tf_op jit(solution)/shard_map/ppermute | solution.py:27
  45.7 50.0 %collective-permute-start.3 = (bf16[1,64,1536]{2,1,0:T(8,128)(2,1)}, bf16[1,64,1536]{2,1,0:T(8,128)(2,1)}, u32[]{:S(2)}, u32[]{:S(2)}) collective-permute-start(bf16[1,64,1536]{2,1,0:T(8,128)(2,1)} %get-tuple-element.109), channel_id=1, source_target_pairs={{1,0},{2,1},{3,2},{4,3},{5,4},{6,5},{7,6},{9,8},{10,9},{11,10},{12... | collective-permute-start | bytes 589832 | tf_op jit(solution)/shard_map/ppermute | solution.py:30
  59.1 85.6 %copy-start.115 = (s32[6]{0:T(128)}, s32[6]{0:T(128)S(1)}, u32[]{:S(2)}) copy-start(s32[6]{0:T(128)S(1)} %dynamic-slice_reduce_fusion.1) | copy-start | bytes 76
  78.6 71.2 %all-to-all-start.1 = ((bf16[8,2,49152]{2,1,0:T(2,128)(2,1)}), bf16[8,2,49152]{2,1,0:T(2,128)(2,1)}, u32[]{:S(2)}, u32[]{:S(2)}) async-start(bf16[8,2,49152]{2,1,0:T(2,128)(2,1)} %reshape.1794), calls=%async_computation.1 | async-start | bytes 3145728 | tf_op jit(solution)/shard_map/all_to_all | solution.py:115
  89.1 176.2 %copy-start.36 = (bf16[2,64,12,64]{1,3,2,0:T(8,128)(2,1)}, bf16[2,64,12,64]{1,3,2,0:T(8,128)(2,1)S(1)}, u32[]{:S(2)}) copy-start(bf16[2,64,12,64]{1,3,2,0:T(8,128)(2,1)S(1)} %copy.339) | copy-start | bytes 589828
  94.4 61.8 %copy-start.117 = (pred[6]{0:T(512)(128)(4,1)}, pred[6]{0:T(512)(128)(4,1)S(1)}, u32[]{:S(2)}) copy-start(pred[6]{0:T(512)(128)(4,1)S(1)} %fusion.147) | copy-start | bytes 22
  272.7 35.2 %copy-start.105 = (f32[128]{0:T(128)}, f32[128]{0:T(128)S(1)}, u32[]{:S(2)}) copy-start(f32[128]{0:T(128)S(1)} %broadcast_multiply_fusion.2) | copy-start | bytes 1540
  273.9 34.1 %copy-start.109 = (f32[128]{0:T(128)}, f32[128]{0:T(128)S(1)}, u32[]{:S(2)}) copy-start(f32[128]{0:T(128)S(1)} %fusion.160) | copy-start | bytes 1540
  279.9 15.0 %slice-start = ((s8[4718592]{0:T(1024)(128)(4,1)}), s8[524288]{0:T(1024)(128)(4,1)S(1)}, s32[]{:S(2)}) async-start(s8[4718592]{0:T(1024)(128)(4,1)} %bitcast.397), calls=%async_computation.7 | async-start | bytes 1048576
  281.7 26.3 %copy-start.16 = (f32[1,128,768]{2,1,0:T(8,128)}, f32[1,128,768]{2,1,0:T(8,128)S(1)}, u32[]{:S(2)}) copy-start(f32[1,128,768]{2,1,0:T(8,128)S(1)} %get-tuple-element.127) | copy-start | bytes 1179652
  281.7 26.3 %copy-start.107 = (f32[128]{0:T(128)}, f32[128]{0:T(128)S(1)}, u32[]{:S(2)}) copy-start(f32[128]{0:T(128)S(1)} %broadcast_multiply_fusion) | copy-start | bytes 1540
  281.9 26.1 %copy-start.111 = (f32[128]{0:T(128)}, f32[128]{0:T(128)S(1)}, u32[]{:S(2)}) copy-start(f32[128]{0:T(128)S(1)} %fusion.162) | copy-start | bytes 1540
  282.0 12.9 %slice-start.1 = ((s8[4718592]{0:T(1024)(128)(4,1)}), s8[4194304]{0:T(1024)(128)(4,1)S(1)}, s32[]{:S(2)}) async-start(s8[4718592]{0:T(1024)(128)(4,1)} %bitcast.397), calls=%async_computation.8 | async-start | bytes 8388608
  310.3 15.3 %copy-start.52 = (bf16[1,128,768]{2,1,0:T(8,128)(2,1)}, bf16[1,128,768]{2,1,0:T(8,128)(2,1)S(1)}, u32[]{:S(2)}) copy-start(bf16[1,128,768]{2,1,0:T(8,128)(2,1)S(1)} %get-tuple-element.105) | copy-start | bytes 589828
  424.7 118.6 %all-to-all-start.2 = ((bf16[8,2,49152]{2,1,0:T(2,128)(2,1)}), bf16[8,2,49152]{2,1,0:T(2,128)(2,1)}, u32[]{:S(2)}, u32[]{:S(2)}) async-start(bf16[8,2,49152]{2,1,0:T(2,128)(2,1)} %reshape.1798), calls=%async_computation.2 | async-start | bytes 3145728 | tf_op jit(solution)/shard_map/all_to_all | solution.py:152
  429.0 109.1 %all-reduce.16.cloned.1.call-start = ((), (), s32[]{:S(2)}) async-start(), calls=%async_computation.5 | async-start | bytes 3145728 | tf_op jit(solution)/shard_map/psum | solution.py:145
  434.0 60.9 %collective-permute-start.5 = (bf16[1,64,1536]{1,2,0:T(8,128)(2,1)}, bf16[1,64,1536]{1,2,0:T(8,128)(2,1)}, u32[]{:S(2)}, u32[]{:S(2)}) collective-permute-start(bf16[1,64,1536]{1,2,0:T(8,128)(2,1)} %bitcast.51), channel_id=1, source_target_pairs={{1,0},{2,1},{3,2},{4,3},{5,4},{6,5},{7,6},{9,8},{10,9},{11,10},{12... | collective-permute-start | bytes 589832 | tf_op jit(solution)/shard_map/ppermute | solution.py:30
  435.3 59.6 %collective-permute-start.4 = (bf16[1,64,1536]{1,2,0:T(8,128)(2,1)}, bf16[1,64,1536]{1,2,0:T(8,128)(2,1)}, u32[]{:S(2)}, u32[]{:S(2)}) collective-permute-start(bf16[1,64,1536]{1,2,0:T(8,128)(2,1)} %bitcast.47), channel_id=1, source_target_pairs={{0,1},{1,2},{2,3},{3,4},{4,5},{5,6},{6,7},{8,9},{9,10},{10,11},{11... | collective-permute-start | bytes 589832 | tf_op jit(solution)/shard_map/ppermute | solution.py:27
  471.3 26.4 %collective-permute-start.7 = (bf16[1,64,1536]{1,2,0:T(8,128)(2,1)}, bf16[1,64,1536]{1,2,0:T(8,128)(2,1)}, u32[]{:S(2)}, u32[]{:S(2)}) collective-permute-start(bf16[1,64,1536]{1,2,0:T(8,128)(2,1)} %bitcast.80), channel_id=1, source_target_pairs={{1,0},{2,1},{3,2},{4,3},{5,4},{6,5},{7,6},{9,8},{10,9},{11,10},{12... | collective-permute-start | bytes 589832 | tf_op jit(solution)/shard_map/ppermute | solution.py:30
  472.6 25.1 %collective-permute-start.6 = (bf16[1,64,1536]{1,2,0:T(8,128)(2,1)}, bf16[1,64,1536]{1,2,0:T(8,128)(2,1)}, u32[]{:S(2)}, u32[]{:S(2)}) collective-permute-start(bf16[1,64,1536]{1,2,0:T(8,128)(2,1)} %bitcast.76), channel_id=1, source_target_pairs={{0,1},{1,2},{2,3},{3,4},{4,5},{5,6},{6,7},{8,9},{9,10},{10,11},{11... | collective-permute-start | bytes 589832 | tf_op jit(solution)/shard_map/ppermute | solution.py:27
  543.2 42.1 %all-to-all-start.3 = ((bf16[8,2,49152]{2,1,0:T(2,128)(2,1)}), bf16[8,2,49152]{2,1,0:T(2,128)(2,1)}, u32[]{:S(2)}, u32[]{:S(2)}) async-start(bf16[8,2,49152]{2,1,0:T(2,128)(2,1)} %reshape.1800), calls=%async_computation.3 | async-start | bytes 3145728 | tf_op jit(solution)/shard_map/all_to_all | solution.py:152
  547.5 495.9 %all-reduce.14.cloned.1.call-start = ((), (), s32[]{:S(2)}) async-start(), calls=%async_computation.4 | async-start | bytes 56623104 | tf_op jit(solution)/shard_map/psum | solution.py:356
  574.1 17.9 %copy-start.124 = (pred[8,2]{0,1:T(4,128)(4,1)S(1)}, pred[8,2]{0,1:T(4,128)(4,1)}, u32[]{:S(2)}) copy-start(pred[8,2]{0,1:T(4,128)(4,1)} %copy-done.123) | copy-start | bytes 52
  631.8 46.1 %copy-start.40 = (f32[1,128,768]{2,1,0:T(8,128)S(1)}, f32[1,128,768]{2,1,0:T(8,128)}, u32[]{:S(2)}) copy-start(f32[1,128,768]{2,1,0:T(8,128)} %copy-done.39) | copy-start | bytes 1179652
  (130 other events, 546.5 us)
Sparse Core Ops, SparseCore 0:
  47.7 83.5 all-reduce.17
  477.1 60.9 all-reduce.15
  608.4 434.9 all-reduce.13
where the time goes:
time: 1090 us; the launch traced here: 1070 us
  waiting for transfers between devices  416 us (38%)
  local copies, waits for them, and re-layouts  330 us (30%)
  matrix products  136 us (12%)
  other arithmetic  82.3 us (8%)
  blocking collectives  51.3 us (5%)
  starting transfers between devices  41.6 us (4%)
  between operations  16 us (1%)
    psum x1, waiting for transfers between devices, body(): lax.psum((gain1_total, shift1_total, query_total, query_bias_total, key_t...  363 us
    unnamed x311, local copies, waits for them, and re-layouts  94.7 us
    concatenate x2, local copies, waits for them, and re-layouts, build_context(): return jnp.concatenate([sliding, global_pair, random_part], axis=2)  59.8 us
    psum x1, blocking collectives, body(): lax.psum((gain1_total, shift1_total, query_total, query_bias_total, key_t...  40.8 us
    dot_general x12, matrix products, weight_grad(): jnp.einsum('wld,wle->de', inputs, gradient, preferred_element_type=jnp.fl...  39.7 us
    psum x1, waiting for transfers between devices, spread_context_grad(): lax.psum(global_part.astype(jnp.bfloat16), 'seq').astype(jnp.float32)  37.7 us
    another operation x16, local copies, waits for them, and re-layouts  37.4 us
    another operation x8, local copies, waits for them, and re-layouts, build_context(): jnp.stack([stacked[:, 0:BLK_DEV], stacked[:, 1:BLK_DEV + 1], stacked[:, 2...  29.5 us
  transfers between devices with their start and end apart: 15, of which 4 were waited for; matrix products, arithmetic and copies ran while one was open for 19% of the time, Pallas kernels for 0%

commit v1 on v0

v1 whole, which is shorter than its diff:
```python
import functools
import math

import jax
import jax.numpy as jnp
from jax import lax
from jax.experimental import pallas as pl
from jax.experimental.pallas import tpu as pltpu
from jax.sharding import PartitionSpec as P

D = 768
HEADS = 12
HEAD_DIM = 64
FF = 3072
BLOCK = 64
RAND = 3
GROUPS = 8
PIECES = 6
ROWS = 1536
STAGES = 9
VEC_ROWS = 16

MESH = pl.DeviceIdType.MESH
VMEM_LIMIT = 60 << 20
epsilon = 1e-05
masked_score = -1e30
score_scale = HEAD_DIM ** (-0.5)
f32 = jnp.float32
bf16 = jnp.bfloat16

whole_vmem = pl.BlockSpec(memory_space=pltpu.VMEM)


def mm(left, right):
    return jnp.dot(left, right, preferred_element_type=f32)


def mm_nt(left, right):
    return lax.dot_general(left, right, (((1,), (1,)), ((), ())), preferred_element_type=f32)


def normalise(v):
    centre = v - jnp.mean(v, axis=-1, keepdims=True)
    rstd = lax.rsqrt(jnp.mean(centre * centre, axis=-1, keepdims=True) + epsilon)
    return centre * rstd, rstd


def norm_back(err, vhat, rstd, gain):
    g = err * gain
    dv = rstd * (
        g - jnp.mean(g, axis=-1, keepdims=True) - vhat * jnp.mean(g * vhat, axis=-1, keepdims=True)
    )
    return dv, jnp.sum(err * vhat, axis=0, keepdims=True), jnp.sum(err, axis=0, keepdims=True)


def plain_call(kernel, outs, scratch=()):
    return pl.pallas_call(
        kernel,
        out_shape=outs,
        scratch_shapes=scratch,
        compiler_params=pltpu.CompilerParams(vmem_limit_bytes=VMEM_LIMIT),
    )


def qkv_kernel(windows, x, gain, shift, wq, bq, wk, wv, bv, qkv, n1_t):
    tokens = x.shape[0] // windows
    vhat, _ = normalise(x[...].astype(f32))
    n1 = (vhat * gain[...] + shift[...]).astype(bf16)
    n1_t[...] = n1.T
    for part, (weight, bias) in enumerate(((wq, bq), (wk, None), (wv, bv))):
        y = mm(n1, weight[...])
        if bias is not None:
            y = y + bias[...]
        y_t = y.astype(bf16).T
        for w in range(windows):
            for h in range(HEADS):
                qkv[w * HEADS + h, part * HEAD_DIM : (part + 1) * HEAD_DIM, :] = y_t[
                    h * HEAD_DIM : (h + 1) * HEAD_DIM, w * tokens : (w + 1) * tokens
                ]
    for p in range(windows * HEADS, qkv.shape[0]):
        qkv[p] = jnp.zeros(qkv.shape[1:], bf16)


def gather_pair(qkv, pair, rows, lanes_t):
    count, tokens = qkv.shape[0], qkv.shape[3]
    for s in range(count):
        lanes_t[:, s * tokens : (s + 1) * tokens] = qkv[s, pair, rows, :]


def query_tile(ref, pair, tile, rows):
    return jnp.concatenate([ref[2 * tile, pair, rows, :], ref[2 * tile + 1, pair, rows, :]], axis=1)


def biased_scores(keys, q_t, bias, pair, lanes):
    length, width = keys.shape[0], q_t.shape[1]
    raw = mm(keys, q_t) * score_scale
    raw = raw.reshape(length // BLOCK, BLOCK // 8, 8, width)
    return (raw + bias[pair, :, :, lanes][:, None]).reshape(length, width)


Q_ROWS, K_ROWS, V_ROWS = (slice(i * HEAD_DIM, (i + 1) * HEAD_DIM) for i in range(3))


def attend_kernel(qkv, bias, out, mass, k_t, v_t):
    count, pairs, _, tokens = qkv.shape
    width = 2 * tokens
    for pair in range(pairs):
        gather_pair(qkv, pair, K_ROWS, k_t)
        gather_pair(qkv, pair, V_ROWS, v_t)
        keys = k_t[...].T

        def one_tile(tile, carry):
            lanes = pl.ds(pl.multiple_of(tile * width, width), width)
            scores = biased_scores(keys, query_tile(qkv, pair, tile, Q_ROWS), bias, pair, lanes)
            top = jnp.max(scores, axis=0, keepdims=True)
            weight = jnp.exp(scores - top)
            total = jnp.sum(weight, axis=0, keepdims=True)
            mass[pair, :, lanes] = top + jnp.log(total)
            probs = (weight * (1.0 / total)).astype(bf16)
            got = mm(v_t[...], probs).astype(bf16)
            out[2 * tile, pair] = got[:, :tokens]
            out[2 * tile + 1, pair] = got[:, tokens:]
            return carry

        lax.fori_loop(0, count // 2, one_tile, 0)


def attend_back_kernel(qkv, bias, mass, grad, out, k_t, v_t, dk, dv):
    count, pairs, _, tokens = qkv.shape
    width = 2 * tokens
    all_rows = slice(0, HEAD_DIM)
    for pair in range(pairs):
        gather_pair(qkv, pair, K_ROWS, k_t)
        gather_pair(qkv, pair, V_ROWS, v_t)
        keys = k_t[...].T
        values = v_t[...].T
        dk[...] = jnp.zeros_like(dk)
        dv[...] = jnp.zeros_like(dv)

        def one_tile(tile, carry):
            lanes = pl.ds(pl.multiple_of(tile * width, width), width)
            q_t = query_tile(qkv, pair, tile, Q_ROWS)
            g_t = query_tile(grad, pair, tile, all_rows)
            scores = biased_scores(keys, q_t, bias, pair, lanes)
            probs = jnp.exp(scores - mass[pair, :, lanes])
            prob_grad = mm(values, g_t)
            row_dot = jnp.sum(probs * prob_grad, axis=0, keepdims=True)
            score_grad = (probs * (prob_grad - row_dot)).astype(bf16)
            dq = (mm(k_t[...], score_grad) * score_scale).astype(bf16)
            out[2 * tile, pair, Q_ROWS, :] = dq[:, :tokens]
            out[2 * tile + 1, pair, Q_ROWS, :] = dq[:, tokens:]
            dk[...] += mm(score_grad, q_t.T)
            dv[...] += mm(probs.astype(bf16), g_t.T)
            return carry

        lax.fori_loop(0, count // 2, one_tile, 0)
        dk_t = (dk[...] * score_scale).astype(bf16).T
        dv_t = dv[...].astype(bf16).T
        for s in range(count):
            out[s, pair, K_ROWS, :] = dk_t[:, s * tokens : (s + 1) * tokens]
            out[s, pair, V_ROWS, :] = dv_t[:, s * tokens : (s + 1) * tokens]


def ffn_kernel(
    windows,
    x,
    att_pairs,
    cot,
    scale,
    wo,
    bo,
    gain,
    shift,
    wup,
    bup,
    wdown,
    bdown,
    y,
    act_t,
    og,
    n2_t,
    pg,
    bg,
    hg,
    do_pairs,
    att_t,
    vec,
):
    tokens = x.shape[0] // windows
    for w in range(windows):
        att_t[:, w * tokens : (w + 1) * tokens] = att_pairs[
            w * HEADS : (w + 1) * HEADS
        ].reshape(D, tokens)
    att = att_t[...].T
    hidden = x[...].astype(f32) + (mm(att, wo[...]) + bo[...])
    vhat, rstd = normalise(hidden)
    n2 = (vhat * gain[...] + shift[...]).astype(bf16)
    n2_t[...] = n2.T
    for w in range(windows):
        rows = slice(w * tokens, (w + 1) * tokens)
        og[rows] = (cot[rows].astype(f32) * scale[w]).astype(bf16)
    out_grad = og[...]
    total = jnp.zeros(hidden.shape, f32)
    err = jnp.zeros(hidden.shape, f32)
    for part in range(FF // D):
        cols = slice(part * D, (part + 1) * D)
        up_part, down_part = wup[:, cols], wdown[cols, :]
        pre = mm(n2, up_part) + bup[:, cols]
        phi = 0.5 * (1.0 + lax.erf(pre * (0.5**0.5)))
        act = (pre * phi).astype(bf16)
        slope = phi + pre * (jnp.exp(-0.5 * pre * pre) * (1.0 / math.sqrt(2.0 * math.pi)))
        act_t[cols, :] = act.T
        total = total + mm(act, down_part)
        grad = (mm_nt(out_grad, down_part) * slope).astype(bf16)
        pg[part] = grad
        vec[8 + part : 9 + part, :] = jnp.sum(grad.astype(f32), axis=0, keepdims=True)
        err = err + mm_nt(grad, up_part)
    y[...] = (hidden + total + bdown[...]).astype(bf16)
    dv, dgain, dshift = norm_back(err, vhat, rstd, gain[...])
    hidden_grad = out_grad.astype(f32) + dv
    hg[...] = hidden_grad
    branch = hidden_grad.astype(bf16)
    bg[...] = branch
    vec[4:5, :] = jnp.sum(branch.astype(f32), axis=0, keepdims=True)
    vec[5:6, :] = dgain
    vec[6:7, :] = dshift
    vec[7:8, :] = jnp.sum(out_grad.astype(f32), axis=0, keepdims=True)
    datt_t = mm_nt(branch, wo[...]).astype(bf16).T
    for w in range(windows):
        do_pairs[w * HEADS : (w + 1) * HEADS] = datt_t[:, w * tokens : (w + 1) * tokens].reshape(
            HEADS, HEAD_DIM, tokens
        )
    for p in range(windows * HEADS, do_pairs.shape[0]):
        do_pairs[p] = jnp.zeros(do_pairs.shape[1:], bf16)


def input_back_kernel(windows, x, gain, grads, hg, wq, wk, wv, dqkv, dx, vec):
    tokens = x.shape[0] // windows
    vhat, rstd = normalise(x[...].astype(f32))
    err = jnp.zeros(vhat.shape, f32)
    for part, weight in enumerate((wq, wk, wv)):
        for w in range(windows):
            grad_t = grads[
                w * HEADS : (w + 1) * HEADS, part * HEAD_DIM : (part + 1) * HEAD_DIM, :
            ].reshape(D, tokens)
            dqkv[part, w * tokens : (w + 1) * tokens, :] = grad_t.T
        grad = dqkv[part]
        err = err + mm_nt(grad, weight[...])
        if part != 1:
            row = 2 + part // 2
            vec[row : row + 1, :] = jnp.sum(grad.astype(f32), axis=0, keepdims=True)
    dv, dgain, dshift = norm_back(err, vhat, rstd, gain[...])
    dx[...] = (hg[...] + dv).astype(bf16)
    vec[0:1, :] = dgain
    vec[1:2, :] = dshift


class Place:
    def __init__(self, layers):
        self.layers = layers
        self.w = lax.axis_index("win")
        self.s = lax.axis_index("seq")
        self.c = lax.rem(self.s, 2)
        self.z = lax.rem(self.s // 2, 4)
        self.layer = self.s // 8
        self.bits = {"a": lax.rem(self.w, 2), "b": self.w // 2}

    def core(self):
        return (self.w, self.s + 1 - 2 * self.c)

    def across(self, axis):
        step = 1 if axis == "a" else 2
        return (self.w + step - 2 * step * self.bits[axis], self.s)

    def along(self, k):
        return (self.w, self.layer * 8 + lax.rem(self.z + k, 4) * 2 + self.c)

    def layer_at(self, k):
        return (self.w, lax.rem(self.layer + k, self.layers) * 8 + self.z * 2 + self.c)

    def peers(self):
        return (
            [self.core(), self.across("a"), self.across("b")]
            + [self.along(k) for k in (1, 2, 3)]
            + [self.layer_at(k) for k in range(1, self.layers)]
        )


def rcopy(src, dst, send, recv, device):
    return pltpu.make_async_remote_copy(
        src, dst, send, recv, device_id=device, device_id_type=MESH
    )


def span(start, size):
    return pl.ds(pl.multiple_of(start, 16), size)


def reduce_piece(place, order, buf, r0, r1, r2, rz, rl, az, send, recv, free):
    c, z = place.c, place.z
    first, second = place.bits[order[0]], place.bits[order[1]]
    half, quarter, eighth, chunk = ROWS // 2, ROWS // 4, ROWS // 8, ROWS // 32
    o0 = c * half
    partners = (place.core(), place.across(order[0]), place.across(order[1]))

    def release(stage):
        pl.semaphore_signal(free.at[stage], inc=1, device_id=partners[stage], device_id_type=MESH)

    cp = rcopy(buf.at[span((1 - c) * half, half)], r0, send.at[0], recv.at[0], place.core())
    cp.start()
    yield
    cp.wait()
    release(0)
    o1, x1 = o0 + first * quarter, o0 + (1 - first) * quarter
    away = span(x1, quarter)
    buf[away] = buf[away] + r0[span((1 - first) * quarter, quarter)]
    cp = rcopy(buf.at[away], r1, send.at[1], recv.at[1], place.across(order[0]))
    cp.start()
    here = span(o1, quarter)
    buf[here] = buf[here] + r0[span(first * quarter, quarter)]
    yield
    cp.wait()
    release(1)
    o2, x2 = o1 + second * eighth, o1 + (1 - second) * eighth
    away = span(x2, eighth)
    buf[away] = buf[away] + r1[span((1 - second) * eighth, eighth)]
    cp = rcopy(buf.at[away], r2, send.at[2], recv.at[2], place.across(order[1]))
    cp.start()
    here = span(o2, eighth)
    buf[here] = buf[here] + r1[span(second * eighth, eighth)]
    yield
    cp.wait()
    release(2)
    here = span(o2, eighth)
    buf[here] = buf[here] + r2[...]

    def chunk_of(k):
        return buf.at[span(o2 + lax.rem(z + k, 4) * chunk, chunk)]

    cps = [
        rcopy(chunk_of(k), rz.at[3 - k], send.at[2 + k], recv.at[6 - k], place.along(k))
        for k in (1, 2, 3)
    ]
    for cp in cps:
        cp.start()
    yield
    for cp in cps:
        cp.wait_send()
    for k in (1, 2, 3):
        rcopy(rz.at[3 - k], rz.at[3 - k], send.at[2 + k], recv.at[6 - k], place.along(k)).wait_recv()
    mine = span(o2 + z * chunk, chunk)
    total = buf[mine].astype(f32)
    for k in range(3):
        total = total + rz[k].astype(f32)
    buf[mine] = total.astype(bf16)
    if place.layers > 1:
        rl[place.layer] = buf[mine]
        cps = [
            rcopy(
                buf.at[mine],
                rl.at[place.layer],
                send.at[11 + k],
                recv.at[11 + place.layers - k],
                place.layer_at(k),
            )
            for k in range(1, place.layers)
        ]
        for cp in cps:
            cp.start()
        for cp in cps:
            cp.wait_send()
        for k in range(1, place.layers):
            slot = rl.at[lax.rem(place.layer + k, place.layers)]
            rcopy(slot, slot, send.at[11 + k], recv.at[11 + k], place.layer_at(k)).wait_recv()
        total = rl[0].astype(f32)
        for k in range(1, place.layers):
            total = total + rl[k].astype(f32)
        buf[mine] = total.astype(bf16)
    cps = [
        rcopy(buf.at[mine], az.at[3 - k], send.at[5 + k], recv.at[9 - k], place.along(k))
        for k in (1, 2, 3)
    ]
    for cp in cps:
        cp.start()
    yield
    for cp in cps:
        cp.wait_send()
    for k in (1, 2, 3):
        slot = az.at[3 - k]
        rcopy(slot, slot, send.at[5 + k], recv.at[9 - k], place.along(k)).wait_recv()
        buf[span(o2 + lax.rem(z + 4 - k, 4) * chunk, chunk)] = az[3 - k]
    for stage, (start, size) in enumerate(((o2, eighth), (o1, quarter), (o0, half))):
        pl.semaphore_wait(free.at[2 - stage], 1)
        held = buf.at[span(start, size)]
        cp = rcopy(held, held, send.at[9 + stage], recv.at[9 + stage], partners[2 - stage])
        cp.start()
        yield
        cp.wait()


def reduce_vectors(place, vec, out, run, got, send, recv):
    run[0] = vec[...]
    for step, device in enumerate((place.core(), place.across("a"), place.across("b"))):
        cp = rcopy(run.at[step], got.at[step], send.at[step], recv.at[step], device)
        cp.start()
        yield
        cp.wait()
        run[step + 1] = run[step] + got[step]
    got[3 + place.z] = run[3]
    cps = [
        rcopy(run.at[3], got.at[3 + place.z], send.at[2 + k], recv.at[6 - k], place.along(k))
        for k in (1, 2, 3)
    ]
    for cp in cps:
        cp.start()
    yield
    for cp in cps:
        cp.wait_send()
    for k in (1, 2, 3):
        slot = got.at[3 + lax.rem(place.z + k, 4)]
        rcopy(slot, slot, send.at[2 + k], recv.at[2 + k], place.along(k)).wait_recv()
    total = got[3]
    for k in range(1, 4):
        total = total + got[3 + k]
    if place.layers > 1:
        run[4] = total
        got[7 + place.layer] = total
        cps = [
            rcopy(
                run.at[4],
                got.at[7 + place.layer],
                send.at[5 + k],
                recv.at[5 + place.layers - k],
                place.layer_at(k),
            )
            for k in range(1, place.layers)
        ]
        for cp in cps:
            cp.start()
        for cp in cps:
            cp.wait_send()
        for k in range(1, place.layers):
            slot = got.at[7 + lax.rem(place.layer + k, place.layers)]
            rcopy(slot, slot, send.at[5 + k], recv.at[5 + k], place.layer_at(k)).wait_recv()
        total = got[7]
        for k in range(1, place.layers):
            total = total + got[7 + k]
    out[...] = total


def grads_kernel(
    layers, act_t, og, n2_t, pg, n1_t, dqkv, att_t, bg, vec, out, vec_out,
    r0, r1, r2, rz, rl, az, send, recv, free, run, got, vec_send, vec_recv,
):
    place = Place(layers)
    barrier = pltpu.get_barrier_semaphore()
    peers = place.peers()
    for peer in peers:
        pl.semaphore_signal(barrier, inc=1, device_id=peer, device_id_type=MESH)
    pl.semaphore_wait(barrier, len(peers))

    def fill(piece, base, left, left_base, right, rows):
        @pl.loop(0, rows // 256)
        def _(i):
            src = span(left_base + i * 256, 256)
            out[piece, span(base + i * 256, 256), :] = mm(left[src, :], right).astype(bf16)

    def compute(piece):
        if piece < 2:
            fill(piece, 0, act_t, piece * ROWS, og[...], ROWS)
        elif piece < 4:
            for j in range(2):
                fill(piece, j * D, n2_t, 0, pg[(piece - 2) * 2 + j], D)
        elif piece == 4:
            for j in range(2):
                fill(piece, j * D, n1_t, 0, dqkv[j], D)
        else:
            fill(piece, 0, n1_t, 0, dqkv[2], D)
            fill(piece, D, att_t, 0, bg[...], D)

    running = [reduce_vectors(place, vec, vec_out, run, got, vec_send, vec_recv)]
    next(running[0])
    for tick in range(PIECES + STAGES):
        fresh = None
        if tick < PIECES:
            compute(tick)
            fresh = reduce_piece(
                place,
                "ab" if tick % 2 == 0 else "ba",
                out.at[tick],
                r0.at[tick],
                r1.at[tick],
                r2.at[tick],
                rz.at[tick],
                rl.at[tick],
                az.at[tick],
                send.at[tick],
                recv.at[tick],
                free.at[tick],
            )
        still = []
        for stream in running:
            if next(stream, True) is None:
                still.append(stream)
        if fresh is not None:
            next(fresh)
            still.append(fresh)
        running = still
    assert not running


def reduce_grads(layers, *operands):
    layer_slots = layers if layers > 1 else 1
    sems = 12 + layers
    return pl.pallas_call(
        functools.partial(grads_kernel, layers),
        out_shape=(
            jax.ShapeDtypeStruct((PIECES, ROWS, D), bf16),
            jax.ShapeDtypeStruct((VEC_ROWS, D), f32),
        ),
        in_specs=[whole_vmem] * 9,
        out_specs=(whole_vmem, whole_vmem),
        scratch_shapes=[
            pltpu.VMEM((PIECES, ROWS // 2, D), bf16),
            pltpu.VMEM((PIECES, ROWS // 4, D), bf16),
            pltpu.VMEM((PIECES, ROWS // 8, D), bf16),
            pltpu.VMEM((PIECES, 3, ROWS // 32, D), bf16),
            pltpu.VMEM((PIECES, layer_slots, ROWS // 32, D), bf16),
            pltpu.VMEM((PIECES, 3, ROWS // 32, D), bf16),
            pltpu.SemaphoreType.DMA((PIECES, sems)),
            pltpu.SemaphoreType.DMA((PIECES, sems)),
            pltpu.SemaphoreType.REGULAR((PIECES, 3)),
            pltpu.VMEM((5, VEC_ROWS, D), f32),
            pltpu.VMEM((7 + layers, VEC_ROWS, D), f32),
            pltpu.SemaphoreType.DMA((6 + layers,)),
            pltpu.SemaphoreType.DMA((6 + layers,)),
        ],
        compiler_params=pltpu.CompilerParams(
            collective_id=0, has_side_effects=True, vmem_limit_bytes=VMEM_LIMIT
        ),
    )(*operands)


def bias_table(random_blocks, blocks, windows_of):
    query = jnp.arange(blocks)[None, :]
    key = jnp.arange(blocks)[:, None]
    fixed = (
        ((key == query - 1) & (query > 0)).astype(f32)
        + (key == query)
        + ((key == query + 1) & (query < blocks - 1))
        + (key == 0)
        + (key == blocks - 1)
    )
    mine = windows_of[:, None, None, None] == jnp.arange(random_blocks.shape[0])[None, :, None, None]
    random_blocks = jnp.sum(jnp.where(mine, random_blocks[None], 0), axis=1)
    picks = jnp.sum(random_blocks[:, None, :, :] == key[None, :, :, None], axis=3)
    count = fixed[None] + picks.astype(f32)
    bias = jnp.where(count > 0, jnp.log(jnp.maximum(count, 1.0)), masked_score)
    bias = jnp.repeat(bias, BLOCK, axis=2)
    return jnp.broadcast_to(bias[:, :, None, :], bias.shape[:2] + (8, bias.shape[2]))


def body(
    tokens,
    cotangent,
    group_ids,
    random_blocks,
    norm1_gain,
    norm1_bias,
    query_weight,
    query_bias,
    key_weight,
    value_weight,
    value_bias,
    out_weight,
    out_bias,
    norm2_gain,
    norm2_bias,
    up_weight,
    up_bias,
    down_weight,
    down_bias,
):
    seq_count = lax.axis_size("seq")
    seq_index = lax.axis_index("seq")
    windows, here, _ = tokens.shape
    length = here * seq_count
    blocks = length // BLOCK
    rows = windows * here
    pairs = -(-windows * HEADS // seq_count)
    slots = pairs * seq_count
    layers = seq_count // 8
    struct = jax.ShapeDtypeStruct

    membership = (group_ids[:, None] == jnp.arange(GROUPS)[None, :]).astype(f32)
    group_sizes = lax.psum(jnp.sum(membership, axis=0), "win")
    window_total = windows * lax.axis_size("win")
    window_scale = window_total / (GROUPS * jnp.sum(membership * group_sizes[None, :], axis=1))

    windows_of = jnp.minimum((seq_index * pairs + jnp.arange(pairs)) // HEADS, windows - 1)
    bias = bias_table(random_blocks, blocks, windows_of)

    def row(v):
        return v.reshape(1, -1)

    x = tokens.reshape(rows, D)
    qkv, n1_t = plain_call(
        functools.partial(qkv_kernel, windows),
        (struct((slots, 3 * HEAD_DIM, here), bf16), struct((D, rows), bf16)),
    )(
        x,
        row(norm1_gain),
        row(norm1_bias),
        query_weight,
        row(query_bias),
        key_weight,
        value_weight,
        row(value_bias),
    )

    def exchange(v):
        v = v.reshape((seq_count, -1) + v.shape[-1:])
        return lax.all_to_all(v, "seq", split_axis=0, concat_axis=0, tiled=True)

    by_head = exchange(qkv).reshape(seq_count, pairs, 3 * HEAD_DIM, here)
    half_lanes = pltpu.VMEM((HEAD_DIM, length), bf16)
    summed = pltpu.VMEM((length, HEAD_DIM), f32)
    attended, mass = plain_call(
        attend_kernel,
        (struct((seq_count, pairs, HEAD_DIM, here), bf16), struct((pairs, 1, length), f32)),
        (half_lanes, half_lanes),
    )(by_head, bias)
    att_pairs = exchange(attended).reshape(slots, HEAD_DIM, here)

    y, act_t, og, n2_t, pg, bg, hg, do_pairs, att_t, vec_b = pl.pallas_call(
        functools.partial(ffn_kernel, windows),
        out_shape=(
            struct((rows, D), bf16),
            struct((FF, rows), bf16),
            struct((rows, D), bf16),
            struct((D, rows), bf16),
            struct((FF // D, rows, D), bf16),
            struct((rows, D), bf16),
            struct((rows, D), f32),
            struct((slots, HEAD_DIM, here), bf16),
            struct((D, rows), bf16),
            struct((VEC_ROWS, D), f32),
        ),
        in_specs=[whole_vmem] * 3 + [pl.BlockSpec(memory_space=pltpu.SMEM)] + [whole_vmem] * 8,
        out_specs=(whole_vmem,) * 10,
        compiler_params=pltpu.CompilerParams(vmem_limit_bytes=VMEM_LIMIT),
    )(
        x,
        att_pairs,
        cotangent.reshape(rows, D),
        window_scale,
        out_weight,
        row(out_bias),
        row(norm2_gain),
        row(norm2_bias),
        up_weight,
        row(up_bias),
        down_weight,
        row(down_bias),
    )

    grad_by_head = exchange(do_pairs).reshape(seq_count, pairs, HEAD_DIM, here)
    back = plain_call(
        attend_back_kernel,
        struct((seq_count, pairs, 3 * HEAD_DIM, here), bf16),
        (half_lanes, half_lanes, summed, summed),
    )(by_head, bias, mass, grad_by_head)
    grad_pairs = exchange(back).reshape(slots, 3 * HEAD_DIM, here)

    dqkv, dx, vec_a = plain_call(
        functools.partial(input_back_kernel, windows),
        (struct((3, rows, D), bf16), struct((rows, D), bf16), struct((VEC_ROWS, D), f32)),
    )(x, row(norm1_gain), grad_pairs, hg, query_weight, key_weight, value_weight)
    vec = jnp.concatenate([vec_a[:4], vec_b[4:12], jnp.zeros((4, D), f32)], axis=0)

    sums, vec_sums = reduce_grads(layers, act_t, og, n2_t, pg, n1_t, dqkv, att_t, bg, vec)
    down_grad = sums[0:2].reshape(FF, D).astype(f32)
    up_grad = sums[2:4].reshape(FF // D, D, D).astype(f32)
    up_grad = jnp.transpose(up_grad, (1, 0, 2)).reshape(D, FF)
    query_grad = sums[4, :D].astype(f32)
    key_grad = sums[4, D:].astype(f32)
    value_grad = sums[5, :D].astype(f32)
    out_grad = sums[5, D:].astype(f32)
    return (
        y.reshape(tokens.shape),
        dx.reshape(tokens.shape),
        vec_sums[0],
        vec_sums[1],
        query_grad,
        vec_sums[2],
        key_grad,
        value_grad,
        vec_sums[3],
        out_grad,
        vec_sums[4],
        vec_sums[5],
        vec_sums[6],
        up_grad,
        vec_sums[8:12].reshape(FF),
        down_grad,
        vec_sums[7],
    )


def solution(mesh):
    split = P("win", "seq", None)
    return jax.shard_map(
        body,
        mesh=mesh,
        in_specs=(split, split, P("win"), P("win", None, None)) + (P(),) * 15,
        out_specs=(split, split) + (P(),) * 15,
        check_vma=False,
    )
```

time: 1090 us -> 392 us (0.36); the launches traced: 1070 us -> 390 us
  waiting for transfers between devices: 416 us -> 57.9 us
  local copies, waits for them, and re-layouts: 330 us -> 28.2 us
  Pallas kernels: 0 us -> 246 us
  matrix products: 136 us -> 0 us
  other arithmetic: 82.3 us -> 16.1 us
  starting transfers between devices: 41.6 us -> 13.3 us
  blocking collectives: 51.3 us -> 27.6 us
  between operations: 16 us -> 0.81 us
    psum x3 -> x0, waiting for transfers between devices: 405 us -> none  [the longest x1 363 us: body(): lax.psum((gain1_total, shift1_total, query_total, query_bias_total, key_t...]
    pallas_call x0 -> x6, Pallas kernels: none -> 246 us  [the longest x1 193 us: reduce_grads(): pl.pallas_call(functools.partial(grads_kernel, layers), out_shape=(jax.Sh...]
    dot_general x56 -> x0, matrix products: 136 us -> none  [the longest x12 39.7 us: weight_grad(): jnp.einsum('wld,wle->de', inputs, gradient, preferred_element_type=jnp.fl...]
    unnamed x311 -> x24, local copies, waits for them, and re-layouts: 94.7 us -> 1.88 us
    another operation x29 -> x0, local copies, waits for them, and re-layouts: 67.3 us -> none
    concatenate x4 -> x1, local copies, waits for them, and re-layouts: 61.8 us -> 0.07 us  [body(): jnp.concatenate([vec_a[:4], vec_b[4:12], jnp.zeros((4, D), f32)], axis=0)]
    all_to_all x4 -> x3, waiting for transfers between devices: 11.3 us -> 57.9 us  [exchange(): return lax.all_to_all(v, 'seq', split_axis=0, concat_axis=0, tiled=True)]
    psum x1 -> x0, blocking collectives: 40.8 us -> none  [body(): lax.psum((gain1_total, shift1_total, query_total, query_bias_total, key_t...]
  transfers between devices with their start and end apart: 15 -> 3, of which waited for: 4 -> 2; matrix products, arithmetic and copies ran while one was open for 19% -> 1% of each run, Pallas kernels for 0% -> 0%
where the time goes in v1:
time: 392 us; the launch traced here: 390 us
  Pallas kernels  246 us (63%)
  waiting for transfers between devices  57.9 us (15%)
  local copies, waits for them, and re-layouts  28.2 us (7%)
  blocking collectives  27.6 us (7%)
  other arithmetic  16.1 us (4%)
  starting transfers between devices  13.3 us (3%)
    pallas_call x1, Pallas kernels, reduce_grads(): pl.pallas_call(functools.partial(grads_kernel, layers), out_shape=(jax.Sh...  193 us
    all_to_all x3, waiting for transfers between devices, exchange(): return lax.all_to_all(v, 'seq', split_axis=0, concat_axis=0, tiled=True)  57.9 us
    all_to_all x1, blocking collectives, exchange(): return lax.all_to_all(v, 'seq', split_axis=0, concat_axis=0, tiled=True)  17.7 us
    pallas_call x1, Pallas kernels, body(): plain_call(attend_back_kernel, struct((seq_count, pairs, 3 * HEAD_DIM, he...  17.5 us
    all_to_all x3, starting transfers between devices, exchange(): return lax.all_to_all(v, 'seq', split_axis=0, concat_axis=0, tiled=True)  13.3 us
    pallas_call x1, Pallas kernels, body(): plain_call(attend_kernel, (struct((seq_count, pairs, HEAD_DIM, here), bf1...  13.3 us
    pallas_call x1, Pallas kernels, body(): pl.pallas_call(functools.partial(ffn_kernel, windows), out_shape=(struct(...  13.1 us
    psum x1, blocking collectives, body(): group_sizes = lax.psum(jnp.sum(membership, axis=0), 'win')  9.89 us
  transfers between devices with their start and end apart: 3, of which 2 were waited for; matrix products, arithmetic and copies ran while one was open for 1% of the time, Pallas kernels for 0%

profile of v1, /device:TPU:0, one launch (start us, length us, event | category | flops | bytes accessed | tf_op | source)
XLA Modules:
  0.0 390.3 jit_solution(3775332503187712740)
XLA Ops:
  0.7 1.3 reshape.311.gain
  1.9 1.3 reshape.312.shift
  3.2 1.3 reshape.313.bq
  4.5 1.3 reshape.314.bv
  5.7 4.5 %shard_map.314 = (bf16[24,192,128]{2,1,0:T(8,128)(2,1)}, bf16[768,256]{1,0:T(8,128)(2,1)}) custom-call(bf16[256,768]{1,0:T(8,128)(2,1)} %bitcast.44, f32[1,768]{1,0:T(1,128)} %reshape.311.gain, f32[1,768]{1,0:T(1,128)} %reshape.312.shift, bf16[768,768]{1,0:T(8,128)(2,1)} %wq.3, f32[1,768]{1,0:T(1,128)} %reshape.313.bq, bf16[768,768]{1,0:T(8,128)(2,1)} %wk.3, ...), custom_call_target="tpu_custom_call" | custom-call | tf_op jit(solution)/shard_map/pallas_call | solution.py:607
  10.3 6.3 %all-to-all-start = ((bf16[8,576,128]{2,1,0:T(8,128)(2,1)}), bf16[8,576,128]{2,1,0:T(8,128)(2,1)S(1)}, u32[]{:S(2)}, u32[]{:S(2)}) async-start(bf16[8,576,128]{2,1,0:T(8,128)(2,1)} %bitcast.49), calls=%async_computation | async-start | bytes 2359296 | tf_op jit(solution)/shard_map/all_to_all | solution.py:623
  17.3 28.7 %all-to-all-done = bf16[8,576,128]{2,1,0:T(8,128)(2,1)S(1)} async-done(((bf16[8,576,128]{2,1,0:T(8,128)(2,1)}), bf16[8,576,128]{2,1,0:T(8,128)(2,1)S(1)}, u32[]{:S(2)}, u32[]{:S(2)}) %all-to-all-start) | async-done | bytes 1179680 | tf_op jit(solution)/shard_map/all_to_all | solution.py:623
  46.0 1.5 broadcast_in_dim.53.bias
  47.5 13.3 %shard_map.315 = (bf16[8,3,64,128]{3,2,1,0:T(8,128)(2,1)}, f32[3,1,1024]{2,1,0:T(1,128)}) custom-call(bf16[8,3,192,128]{3,2,1,0:T(8,128)(2,1)} %bitcast.39, f32[3,16,8,1024]{3,2,1,0:T(8,128)} %broadcast_in_dim.53.bias), custom_call_target="tpu_custom_call" | custom-call | tf_op jit(solution)/shard_map/pallas_call | solution.py:628
  60.8 3.5 all-to-all-start.1
  64.4 9.9 %psum.7 = f32[8]{0:T(128)S(1)} all-reduce(f32[8]{0:T(128)S(1)} %convert_reduce_fusion.1), channel_id=1, replica_groups=mesh['win'=4,'seq'=8] {'win'}, use_global_device_ids=true, to_apply=%region_3.4 | all-reduce | flops 8 | bytes 64 | tf_op jit(solution)/shard_map/psum | solution.py:596
  74.3 0.6 reshape.320.bo
  74.9 0.6 reshape.321.gain
  77.3 0.7 copy-done.2
  78.1 13.1 %shard_map.316 = (bf16[256,768]{1,0:T(8,128)(2,1)}, bf16[3072,256]{1,0:T(8,128)(2,1)}, bf16[256,768]{1,0:T(8,128)(2,1)}, bf16[768,256]{1,0:T(8,128)(2,1)}, bf16[...) custom-call(bf16[256,768]{1,0:T(8,128)(2,1)} %bitcast.45, ...), custom_call_target="tpu_custom_call" | custom-call | tf_op jit(solution)/shard_map/pallas_call | solution.py:635
  91.2 17.7 %all_to_all.20 = bf16[8,192,128]{2,1,0:T(8,128)(2,1)} all-to-all(bf16[8,192,128]{2,1,0:T(8,128)(2,1)} %bitcast.51), channel_id=1, replica_groups=mesh['win'=4,'seq'=8] {'seq'}, dimensions={0} | all-to-all | bytes 786432 | tf_op jit(solution)/shard_map/all_to_all | solution.py:623
  108.8 17.5 %shard_map.317 = bf16[8,3,192,128]{3,2,1,0:T(8,128)(2,1)} custom-call(bf16[8,3,192,128]{3,2,1,0:T(8,128)(2,1)} %bitcast.40, f32[3,16,8,1024]{3,2,1,0:T(8,128)} %broadcast_in_dim.53.bias, f32[3,1,1024]{2,1,0:T(1,128)} %get-tuple-element.39.mass, bf16[8,3,64,128]{3,2,1,0:T(8,128)(2,1)} %bitcast.47), custom_call_target="tpu_custom_call" | custom-call | tf_op jit(solution)/shard_map/pallas_call | solution.py:668
  126.4 3.6 all-to-all-start.3
  130.1 29.2 %all-to-all-done.3 = bf16[8,576,128]{2,1,0:T(8,128)(2,1)S(1)} async-done(((bf16[8,576,128]{2,1,0:T(8,128)(2,1)}), bf16[8,576,128]{2,1,0:T(8,128)(2,1)S(1)}, u32[]{:S(2)}, u32[]{:S(2)}) %all-to-all-start.3) | async-done | bytes 1179680 | tf_op jit(solution)/shard_map/all_to_all | solution.py:623
  159.3 1.0 copy-done.1
  160.3 4.9 %shard_map.318 = (bf16[3,256,768]{2,1,0:T(8,128)(2,1)}, bf16[256,768]{1,0:T(8,128)(2,1)}, f32[16,768]{1,0:T(8,128)}) custom-call(bf16[256,768]{1,0:T(8,128)(2,1)} %bitcast.46, f32[1,768]{1,0:T(1,128)} %reshape.311.gain, bf16[24,192,128]{2,1,0:T(8,128)(2,1)} %bitcast.43, f32[256,768]{1,0:T(8,128)} %get-tuple-element.41.hg, bf16[768,768]{1,0:T(8,128)(2,1)} %wq.3, ...), custom_call_target="tpu_custom_call" | custom-call | tf_op jit(solution)/shard_map/pallas_call | solution.py:675
  165.2 0.7 slice.51
  165.9 0.7 maximum_maximum_fusion.vec
  166.6 193.0 %shard_map.319 = (bf16[6,1536,768]{2,1,0:T(8,128)(2,1)}, f32[16,768]{1,0:T(8,128)}) custom-call(bf16[3072,256]{1,0:T(8,128)(2,1)} %get-tuple-element.43.act_t, bf16[256,768]{1,0:T(8,128)(2,1)} %get-tuple-element.44.og, bf16[768,256]{1,0:T(8,128)(2,1)} %get-tuple-element.45.n2_t, bf16[4,256,768]{2,1,0:T(8,128)(2,1)} %get-tuple-element.46.pg, ...), custom_call_target="tpu_custom_call" | custom-call | tf_op jit(solution)/shard_map/pallas_call | solution.py:515
  359.6 0.7 slice.65
  360.4 1.7 slice_reduce_fusion
  362.1 6.2 %bitcast_convert_fusion.1 = (f32[768,768]{1,0:T(8,128)}, f32[768,768]{1,0:T(8,128)}, f32[768,768]{1,0:T(8,128)}, f32[768,768]{1,0:T(8,128)}) fusion(bf16[6,1536,768]{2,1,0:T(8,128)(2,1)} %get-tuple-element.54), kind=kLoop, calls=%fused_computation.2 | loop fusion | flops 2359296 | bytes 14155776 | tf_op jit(solution)/shard_map/convert_element_type | solution.py:688
  368.3 8.1 %fusion.3 = (bf16[2,1536,768]{2,1,0:T(8,128)(2,1)}, bf16[2,1536,768]{2,1,0:T(8,128)(2,1)}) fusion(bf16[6,1536,768]{2,1,0:T(8,128)(2,1)} %get-tuple-element.54), kind=kLoop, calls=%fused_computation.39 | loop fusion | bytes 18874368 | tf_op jit(solution)/shard_map/slice | solution.py:682
  376.4 0.6 reshape.333
  377.0 3.3 convert_bitcast_fusion
  380.3 5.2 %copy.39 = f32[4,96,8,768]{3,2,0,1:T(8,128)} copy(f32[4,96,8,768]{3,2,1,0:T(8,128)S(1)} %convert_bitcast_fusion) | data formatting | bytes 18874368 | tf_op jit(solution)/shard_map/reshape | solution.py:684
  385.5 4.8 %bitcast_convert_fusion = f32[3072,768]{1,0:T(8,128)} fusion(bf16[2,1536,768]{2,1,0:T(8,128)(2,1)S(1)} %bitcast.37), kind=kLoop, calls=%fused_computation.1 | loop fusion | flops 2359296 | bytes 14155776 | tf_op jit(solution)/shard_map/convert_element_type | solution.py:682
  (43 shorter events, 2.8 us)
Async XLA Ops:
  5.7 11.0 %copy-start.8 = (s32[2,16,3]{1,0,2:T(2,128)S(1)}, s32[2,16,3]{1,0,2:T(2,128)}, u32[]{:S(2)}) copy-start(s32[2,16,3]{1,0,2:T(2,128)} %param.22) | copy-start | bytes 1156
  10.3 35.7 %all-to-all-start = ((bf16[8,576,128]{2,1,0:T(8,128)(2,1)}), bf16[8,576,128]{2,1,0:T(8,128)(2,1)S(1)}, u32[]{:S(2)}, u32[]{:S(2)}) async-start(bf16[8,576,128]{2,1,0:T(8,128)(2,1)} %bitcast.49), calls=%async_computation | async-start | bytes 2359296 | tf_op jit(solution)/shard_map/all_to_all | solution.py:623
  17.3 47.0 %copy-start.9 = (s32[2]{0:T(128)S(1)}, s32[2]{0:T(128)}, u32[]{:S(2)}) copy-start(s32[2]{0:T(128)} %param.21) | copy-start | bytes 28
  17.3 57.0 %copy-start.4 = (f32[768]{0:T(1024)S(1)}, f32[768]{0:T(1024)}, u32[]{:S(2)}) copy-start(f32[768]{0:T(1024)} %param.31) | copy-start | bytes 9220
  17.3 57.6 %copy-start.5 = (f32[768]{0:T(1024)S(1)}, f32[768]{0:T(1024)}, u32[]{:S(2)}) copy-start(f32[768]{0:T(1024)} %param.32) | copy-start | bytes 9220
  17.3 58.2 %copy-start.6 = (f32[768]{0:T(1024)S(1)}, f32[768]{0:T(1024)}, u32[]{:S(2)}) copy-start(f32[768]{0:T(1024)} %param.33) | copy-start | bytes 9220
  17.3 58.7 %copy-start.7 = (f32[768]{0:T(1024)S(1)}, f32[768]{0:T(1024)}, u32[]{:S(2)}) copy-start(f32[768]{0:T(1024)} %param.37) | copy-start | bytes 9220
  46.0 1.5 copy-start
  60.8 16.5 %all-to-all-start.1 = ((bf16[8,192,128]{2,1,0:T(8,128)(2,1)}), bf16[8,192,128]{2,1,0:T(8,128)(2,1)S(1)}, u32[]{:S(2)}, u32[]{:S(2)}) async-start(bf16[8,192,128]{2,1,0:T(8,128)(2,1)} %bitcast.50), calls=%async_computation.1 | async-start | bytes 786432 | tf_op jit(solution)/shard_map/all_to_all | solution.py:623
  77.3 0.7 copy-start.2
  108.8 21.2 %copy-start.3 = (f32[16,768]{1,0:T(8,128)S(1)}, f32[16,768]{1,0:T(8,128)}, u32[]{:S(2)}) copy-start(f32[16,768]{1,0:T(8,128)} %get-tuple-element.52) | copy-start | bytes 147460
  126.4 32.9 %all-to-all-start.3 = ((bf16[8,576,128]{2,1,0:T(8,128)(2,1)}), bf16[8,576,128]{2,1,0:T(8,128)(2,1)S(1)}, u32[]{:S(2)}, u32[]{:S(2)}) async-start(bf16[8,576,128]{2,1,0:T(8,128)(2,1)} %bitcast.42), calls=%async_computation.3 | async-start | bytes 2359296 | tf_op jit(solution)/shard_map/all_to_all | solution.py:623
  159.3 1.0 copy-start.1
  377.0 8.5 %slice-start = ((s8[4718592]{0:T(1024)(128)(4,1)}), s8[4194304]{0:T(1024)(128)(4,1)S(1)}, s32[]{:S(2)}) async-start(s8[4718592]{0:T(1024)(128)(4,1)} %bitcast.36), calls=%async_computation.4 | async-start | bytes 8388608
  380.3 5.2 %slice-start.1 = ((s8[4718592]{0:T(1024)(128)(4,1)}), s8[524288]{0:T(1024)(128)(4,1)S(1)}, s32[]{:S(2)}) async-start(s8[4718592]{0:T(1024)(128)(4,1)} %bitcast.36), calls=%async_computation.5 | async-start | bytes 1048576

commit v2 on v1

v2 whole, which is shorter than its diff:
```python
import functools
import math

import jax
import jax.numpy as jnp
from jax import lax
from jax.experimental import pallas as pl
from jax.experimental.pallas import tpu as pltpu
from jax.sharding import PartitionSpec as P

D = 768
HEADS = 12
HEAD_DIM = 64
FF = 3072
BLOCK = 64
RAND = 3
GROUPS = 8
TILES = FF // D
VEC_ROWS = 16
OWN = 6
HALF = D // 2

MESH = pl.DeviceIdType.MESH
VMEM_LIMIT = 60 << 20
epsilon = 1e-05
masked_score = -1e30
score_scale = HEAD_DIM ** (-0.5)
f32 = jnp.float32
bf16 = jnp.bfloat16

in_vmem = pl.BlockSpec(memory_space=pltpu.VMEM)
in_smem = pl.BlockSpec(memory_space=pltpu.SMEM)
anywhere = pl.BlockSpec(memory_space=pl.ANY)


def mm(left, right):
    return jnp.dot(left, right, preferred_element_type=f32)


def mm_nt(left, right):
    return lax.dot_general(left, right, (((1,), (1,)), ((), ())), preferred_element_type=f32)


def row(ref):
    return ref[...].reshape(1, -1)


def normalise(v):
    centre = v - jnp.mean(v, axis=-1, keepdims=True)
    rstd = lax.rsqrt(jnp.mean(centre * centre, axis=-1, keepdims=True) + epsilon)
    return centre * rstd, rstd


def norm_back(err, vhat, rstd, gain):
    g = err * gain
    dv = rstd * (
        g - jnp.mean(g, axis=-1, keepdims=True) - vhat * jnp.mean(g * vhat, axis=-1, keepdims=True)
    )
    return dv, jnp.sum(err * vhat, axis=0, keepdims=True), jnp.sum(err, axis=0, keepdims=True)


def rcopy(src, dst, send, recv, device):
    return pltpu.make_async_remote_copy(
        src, dst, send, recv, device_id=device, device_id_type=MESH
    )


def span(start, size):
    return pl.ds(pl.multiple_of(start, 16), size)


class Place:
    def __init__(self, wins, seqs):
        self.wins, self.seqs = wins, seqs
        self.layers = seqs // 8
        self.w = lax.axis_index("win")
        self.s = lax.axis_index("seq")
        self.c = lax.rem(self.s, 2)
        self.z = lax.rem(self.s // 2, 4)
        self.layer = self.s // 8
        self.bits = {"a": lax.rem(self.w, 2), "b": self.w // 2}

    def core(self):
        return (self.w, self.s + 1 - 2 * self.c)

    def across(self, axis):
        step = 1 if axis == "a" else 2
        return (self.w + step - 2 * step * self.bits[axis], self.s)

    def along(self, k):
        return (self.w, self.layer * 8 + lax.rem(self.z + k, 4) * 2 + self.c)

    def layer_at(self, k):
        return (self.w, lax.rem(self.layer + k, self.layers) * 8 + self.z * 2 + self.c)

    def seq_at(self, k):
        return lax.rem(self.s + k, self.seqs)

    def win_at(self, k):
        return (lax.rem(self.w + k, self.wins), self.s)

    def greet(self, across_win):
        barrier = pltpu.get_barrier_semaphore()

        def one(k, carry):
            pl.semaphore_signal(
                barrier, inc=1, device_id=(self.w, self.seq_at(k)), device_id_type=MESH
            )
            return carry

        lax.fori_loop(1, self.seqs, one, 0)
        for peer in across_win:
            pl.semaphore_signal(barrier, inc=1, device_id=peer, device_id_type=MESH)
        return barrier, self.seqs - 1 + len(across_win)


class Exchange:
    def __init__(self, place, pairs, out, into, send, recv):
        self.place, self.pairs = place, pairs
        self.out, self.into, self.send, self.recv = out, into, send, recv

    def copy(self, k, pair):
        place = self.place
        target = place.seq_at(k)
        return rcopy(
            self.out.at[target * self.pairs + pair],
            self.into.at[place.s, pair],
            self.send.at[k, pair],
            self.recv.at[k, pair],
            (place.w, target),
        )

    def start(self, pair):
        def one(k, carry):
            self.copy(k, pair).start()
            return carry

        lax.fori_loop(1, self.place.seqs, one, 0)
        self.into[self.place.s, pair] = self.out[self.place.s * self.pairs + pair]

    def arrived(self, pair):
        def one(k, carry):
            place = self.place
            slot = self.into.at[lax.rem(place.s + place.seqs - k, place.seqs), pair]
            rcopy(
                slot, slot, self.send.at[k, pair], self.recv.at[k, pair], (place.w, place.seq_at(k))
            ).wait_recv()
            return carry

        lax.fori_loop(1, self.place.seqs, one, 0)

    def sent(self, pair):
        def one(k, carry):
            self.copy(k, pair).wait_send()
            return carry

        lax.fori_loop(1, self.place.seqs, one, 0)


Q_ROWS, K_ROWS, V_ROWS = (slice(i * HEAD_DIM, (i + 1) * HEAD_DIM) for i in range(3))


def tile_width(length):
    return 256 if length <= 2048 else 128


def block_ones(keys_t, blocks):
    rows, length = keys_t.shape
    shape = (rows - HEAD_DIM, length)
    part = lax.broadcasted_iota(jnp.int32, shape, 0)
    block = lax.broadcasted_iota(jnp.int32, shape, 1) // BLOCK
    hit = (part == block) | (part == block + blocks) | (part == block + 2 * blocks)
    keys_t[HEAD_DIM:, :] = jnp.where(hit, 1.0, 0.0).astype(bf16)


def gather_rows(ref, pair, rows, into):
    tokens = ref.shape[3]
    for s in range(ref.shape[0]):
        into[: rows.stop - rows.start, s * tokens : (s + 1) * tokens] = ref[s, pair, rows, :]


def query_tile(ref, pair, tile, rows, width):
    parts = width // ref.shape[3]
    return jnp.concatenate([ref[parts * tile + i, pair, rows, :] for i in range(parts)], axis=1)


def put_tile(ref, pair, tile, rows, value, slot):
    tokens = value.shape[1]
    tokens = ref.shape[-1]
    parts = value.shape[1] // tokens
    for i in range(parts):
        ref[slot(parts * tile + i, pair) + (rows,)] = value[:, i * tokens : (i + 1) * tokens]


def biased_scores(keys, q_t, bias, pair, lanes):
    return mm(keys, jnp.concatenate([q_t, bias[pair, :, lanes]], axis=0))


def attend_pair(pair, qkv, bias, keys_t, v_t, put, mass):
    length = v_t.shape[1]
    width = tile_width(length)
    gather_rows(qkv, pair, K_ROWS, keys_t)
    gather_rows(qkv, pair, V_ROWS, v_t)
    keys = keys_t[...].T

    def one_tile(tile, carry):
        lanes = pl.ds(pl.multiple_of(tile * width, width), width)
        scores = biased_scores(keys, query_tile(qkv, pair, tile, Q_ROWS, width), bias, pair, lanes)
        top = jnp.max(scores, axis=0, keepdims=True)
        weight = jnp.exp(scores - top)
        total = jnp.sum(weight, axis=0, keepdims=True)
        mass[pair, :, lanes] = top + jnp.log(total)
        probs = (weight * (1.0 / total)).astype(bf16)
        put(tile, pair, mm(v_t[...], probs).astype(bf16))
        return carry

    lax.fori_loop(0, length // width, one_tile, 0)


def attend_pair_back(pair, qkv, grad, bias, mass, keys_t, v_t, dk, dv, put, finish):
    length = v_t.shape[1]
    width = tile_width(length)
    gather_rows(qkv, pair, K_ROWS, keys_t)
    gather_rows(qkv, pair, V_ROWS, v_t)
    keys = keys_t[...].T
    values = v_t[...].T
    dk[...] = jnp.zeros_like(dk)
    dv[...] = jnp.zeros_like(dv)

    def one_tile(tile, carry):
        lanes = pl.ds(pl.multiple_of(tile * width, width), width)
        q_t = query_tile(qkv, pair, tile, Q_ROWS, width)
        g_t = query_tile(grad, pair, tile, slice(0, HEAD_DIM), width)
        scores = biased_scores(keys, q_t, bias, pair, lanes)
        probs = jnp.exp(scores - mass[pair, :, lanes])
        prob_grad = mm(values, g_t)
        row_dot = jnp.sum(probs * prob_grad, axis=0, keepdims=True)
        score_grad = (probs * (prob_grad - row_dot)).astype(bf16)
        put(tile, pair, (mm(keys_t[:HEAD_DIM, :], score_grad) * score_scale).astype(bf16))
        dk[...] += mm(score_grad, q_t.T)
        dv[...] += mm(probs.astype(bf16), g_t.T)
        return carry

    lax.fori_loop(0, length // width, one_tile, 0)
    finish(pair, dk[...].astype(bf16).T, dv[...].astype(bf16).T)


def project_qkv(x, gain, shift, wq, bq, wk, wv, bv, out, n1_t, windows):
    tokens = x.shape[0] // windows
    vhat, _ = normalise(x[...].astype(f32))
    n1 = (vhat * row(gain) + row(shift)).astype(bf16)
    n1_t[...] = n1.T
    for part, (weight, bias) in enumerate(((wq, bq), (wk, None), (wv, bv))):
        y = mm(n1, weight[...])
        if bias is not None:
            y = y + row(bias)
        y = y.astype(bf16)
        if part == 0:
            y = y * jnp.asarray(score_scale, bf16)
        y_t = y.T
        for w in range(windows):
            for h in range(HEADS):
                out[w * HEADS + h, part * HEAD_DIM : (part + 1) * HEAD_DIM, :] = y_t[
                    h * HEAD_DIM : (h + 1) * HEAD_DIM, w * tokens : (w + 1) * tokens
                ]
    for p in range(windows * HEADS, out.shape[0]):
        out[p] = jnp.zeros(out.shape[1:], bf16)


def feed_forward(
    x, att_t, cot, scales, wo, bo, gain, shift, wup, bup, wdown, bdown,
    y, act_t, og, n2_t, pg, bg, hg, do_out, vec,
):
    windows = len(scales)
    tokens = x.shape[0] // windows
    hidden = x[...].astype(f32) + (mm(att_t[...].T, wo[...]) + row(bo))
    vhat, rstd = normalise(hidden)
    n2 = (vhat * row(gain) + row(shift)).astype(bf16)
    n2_t[...] = n2.T
    for w in range(windows):
        rows = slice(w * tokens, (w + 1) * tokens)
        og[rows] = (cot[rows].astype(f32) * scales[w]).astype(bf16)
    out_grad = og[...]
    total = jnp.zeros(hidden.shape, f32)
    err = jnp.zeros(hidden.shape, f32)
    up_bias = row(bup)
    for part in range(TILES):
        cols = slice(part * D, (part + 1) * D)
        up_part, down_part = wup[:, cols], wdown[cols, :]
        pre = mm(n2, up_part) + up_bias[:, cols]
        phi = 0.5 * (1.0 + lax.erf(pre * (0.5**0.5)))
        act = (pre * phi).astype(bf16)
        slope = phi + pre * (jnp.exp(-0.5 * pre * pre) * (1.0 / math.sqrt(2.0 * math.pi)))
        act_t[part] = act.T
        total = total + mm(act, down_part)
        grad = (mm_nt(out_grad, down_part) * slope).astype(bf16)
        pg[part] = grad
        vec[8 + part : 9 + part, :] = jnp.sum(grad.astype(f32), axis=0, keepdims=True)
        err = err + mm_nt(grad, up_part)
    y[...] = (hidden + total + row(bdown)).astype(bf16)
    dv, dgain, dshift = norm_back(err, vhat, rstd, row(gain))
    hidden_grad = out_grad.astype(f32) + dv
    hg[...] = hidden_grad
    branch = hidden_grad.astype(bf16)
    bg[...] = branch
    vec[4:5, :] = jnp.sum(branch.astype(f32), axis=0, keepdims=True)
    vec[5:6, :] = dgain
    vec[6:7, :] = dshift
    vec[7:8, :] = jnp.sum(out_grad.astype(f32), axis=0, keepdims=True)
    vec[0:4, :] = jnp.zeros((4, D), f32)
    vec[12:16, :] = jnp.zeros((4, D), f32)
    datt_t = mm_nt(branch, wo[...]).astype(bf16).T
    for w in range(windows):
        do_out[w * HEADS : (w + 1) * HEADS] = datt_t[:, w * tokens : (w + 1) * tokens].reshape(
            HEADS, HEAD_DIM, tokens
        )
    for p in range(windows * HEADS, do_out.shape[0]):
        do_out[p] = jnp.zeros(do_out.shape[1:], bf16)


def forward_kernel(
    dims,
    ids, x, gain1, shift1, wq, bq, wk, wv, bv, bias, cot_hbm, wo_hbm, bo, gain2, shift2,
    wup_hbm, bup, wdown_hbm, bdown,
    y, by_head, mass, act_t, og, n2_t, pg, bg, hg, do_out, att_t, n1_t, vec,
    qkv_out, att_out, att_in, keys_t, v_t, counts, cot, wo, wup, wdown,
    load, qkv_send, qkv_recv, att_send, att_recv, count_send, count_recv,
):
    wins, seqs, windows, pairs = dims
    place = Place(wins, seqs)
    loads = [
        pltpu.make_async_copy(src, dst, load.at[i])
        for i, (src, dst) in enumerate(
            ((wo_hbm, wo), (cot_hbm, cot), (wup_hbm, wup), (wdown_hbm, wdown))
        )
    ]
    for copy in loads:
        copy.start()
    barrier, expected = place.greet([place.win_at(k) for k in range(1, wins)])
    project_qkv(x, gain1, shift1, wq, bq, wk, wv, bv, qkv_out, n1_t, windows)
    lane = lax.broadcasted_iota(jnp.int32, (8, 128), 1)
    member = [(lane == ids[w]).astype(f32) for w in range(windows)]
    counts[place.w] = sum(member[1:], member[0])
    pl.semaphore_wait(barrier, expected)

    qkv_moves = Exchange(place, pairs, qkv_out, by_head, qkv_send, qkv_recv)
    for pair in range(pairs):
        qkv_moves.start(pair)
    mine = counts.at[place.w]
    count_moves = [
        rcopy(mine, mine, count_send.at[k], count_recv.at[k], place.win_at(k))
        for k in range(1, wins)
    ]
    for copy in count_moves:
        copy.start()

    block_ones(keys_t, v_t.shape[1] // BLOCK)
    att_moves = Exchange(place, pairs, att_out, att_in, att_send, att_recv)

    def put(tile, pair, value):
        tokens = att_out.shape[-1]
        parts = value.shape[1] // tokens
        for i in range(parts):
            att_out[(tile * parts + i) * pairs + pair] = value[:, i * tokens : (i + 1) * tokens]

    for pair in range(pairs):
        qkv_moves.arrived(pair)
        attend_pair(pair, by_head, bias, keys_t, v_t, put, mass)
        att_moves.start(pair)

    for copy in count_moves:
        copy.wait_send()
    for k in range(1, wins):
        slot = counts.at[lax.rem(place.w + wins - k, wins)]
        rcopy(slot, slot, count_send.at[k], count_recv.at[k], place.win_at(k)).wait_recv()
    sizes = counts[0]
    for k in range(1, wins):
        sizes = sizes + counts[k]
    first_row = lax.broadcasted_iota(jnp.int32, (8, 128), 0) == 0
    scales = []
    for w in range(windows):
        own_size = jnp.sum(jnp.where(first_row, member[w] * sizes, 0.0), keepdims=True)
        scales.append(windows * wins / (GROUPS * own_size))

    for pair in range(pairs):
        att_moves.arrived(pair)
    tokens = x.shape[0] // windows
    for w in range(windows):
        for h in range(HEADS):
            slot, pair = divmod(w * HEADS + h, pairs)
            att_t[h * HEAD_DIM : (h + 1) * HEAD_DIM, w * tokens : (w + 1) * tokens] = att_in[
                slot, pair
            ]
    for copy in loads:
        copy.wait()
    feed_forward(
        x, att_t, cot, scales, wo, bo, gain2, shift2, wup, bup, wdown, bdown,
        y, act_t, og, n2_t, pg, bg, hg, do_out, vec,
    )
    for pair in range(pairs):
        qkv_moves.sent(pair)
        att_moves.sent(pair)


def reduce_halves(place, out, index, j, r1, r2, rz, rl, az, send, recv, free):
    parts = [
        reduce_half(
            place, order, out.at[index], h * HALF,
            *(ref.at[2 * j + h] for ref in (r1, r2, rz, rl, az, send, recv, free)),
        )
        for h, order in enumerate(("ab", "ba"))
    ]
    while True:
        alive = [next(part, True) is None for part in parts]
        if not any(alive):
            break
        yield
    held = out.at[index]
    cp = rcopy(held, held, send.at[2 * j, 8], recv.at[2 * j, 8], place.core())
    cp.start()
    yield
    cp.wait()


def reduce_half(place, order, buf, col, r1, r2, rz, rl, az, send, recv, free):
    z = place.z
    cols = pl.ds(col, HALF)
    first, second = place.bits[order[0]], place.bits[order[1]]
    quarter, eighth, chunk = D // 2, D // 4, D // 16
    partners = (place.across(order[0]), place.across(order[1]))

    def at(start, size):
        return buf.at[span(start, size), cols]

    def release(stage):
        pl.semaphore_signal(free.at[stage], inc=1, device_id=partners[stage], device_id_type=MESH)

    o1, x1 = first * quarter, (1 - first) * quarter
    cp = rcopy(at(x1, quarter), r1, send.at[0], recv.at[0], partners[0])
    cp.start()
    yield
    cp.wait()
    release(0)
    o2, x2 = o1 + second * eighth, o1 + (1 - second) * eighth
    at(x2, eighth)[...] = at(x2, eighth)[...] + r1[span((1 - second) * eighth, eighth)]
    cp = rcopy(at(x2, eighth), r2, send.at[1], recv.at[1], partners[1])
    cp.start()
    at(o2, eighth)[...] = at(o2, eighth)[...] + r1[span(second * eighth, eighth)]
    yield
    cp.wait()
    release(1)
    at(o2, eighth)[...] = at(o2, eighth)[...] + r2[...]

    def chunk_of(k):
        return at(o2 + lax.rem(z + k, 4) * chunk, chunk)

    cps = [
        rcopy(chunk_of(k), rz.at[3 - k], send.at[1 + k], recv.at[5 - k], place.along(k))
        for k in (1, 2, 3)
    ]
    for cp in cps:
        cp.start()
    yield
    for cp in cps:
        cp.wait_send()
    for k in (1, 2, 3):
        rcopy(rz.at[3 - k], rz.at[3 - k], send.at[1 + k], recv.at[5 - k], place.along(k)).wait_recv()
    mine = at(o2 + z * chunk, chunk)
    total = mine[...].astype(f32)
    for k in range(3):
        total = total + rz[k].astype(f32)
    mine[...] = total.astype(bf16)
    layers = place.layers
    if layers > 1:
        rl[place.layer] = mine[...]
        cps = [
            rcopy(
                mine, rl.at[place.layer], send.at[10 + k], recv.at[10 + layers - k],
                place.layer_at(k),
            )
            for k in range(1, layers)
        ]
        for cp in cps:
            cp.start()
        for cp in cps:
            cp.wait_send()
        for k in range(1, layers):
            slot = rl.at[lax.rem(place.layer + k, layers)]
            rcopy(slot, slot, send.at[10 + k], recv.at[10 + k], place.layer_at(k)).wait_recv()
        total = rl[0].astype(f32)
        for k in range(1, layers):
            total = total + rl[k].astype(f32)
        mine[...] = total.astype(bf16)
    cps = [
        rcopy(mine, az.at[3 - k], send.at[4 + k], recv.at[8 - k], place.along(k)) for k in (1, 2, 3)
    ]
    for cp in cps:
        cp.start()
    yield
    for cp in cps:
        cp.wait_send()
    for k in (1, 2, 3):
        slot = az.at[3 - k]
        rcopy(slot, slot, send.at[4 + k], recv.at[8 - k], place.along(k)).wait_recv()
        at(o2 + lax.rem(z + 4 - k, 4) * chunk, chunk)[...] = slot[...]
    for stage, start, size in ((1, o2, eighth), (0, o1, quarter)):
        pl.semaphore_wait(free.at[stage], 1)
        held = at(start, size)
        cp = rcopy(held, held, send.at[10 - stage], recv.at[10 - stage], partners[stage])
        cp.start()
        yield
        cp.wait()


def reduce_vectors(place, out, run, got, send, recv):
    for step, device in enumerate((place.core(), place.across("a"), place.across("b"))):
        cp = rcopy(run.at[step], got.at[step], send.at[step], recv.at[step], device)
        cp.start()
        yield
        cp.wait()
        run[step + 1] = run[step] + got[step]
    got[3 + place.z] = run[3]
    cps = [
        rcopy(run.at[3], got.at[3 + place.z], send.at[2 + k], recv.at[6 - k], place.along(k))
        for k in (1, 2, 3)
    ]
    for cp in cps:
        cp.start()
    yield
    for cp in cps:
        cp.wait_send()
    for k in (1, 2, 3):
        slot = got.at[3 + lax.rem(place.z + k, 4)]
        rcopy(slot, slot, send.at[2 + k], recv.at[2 + k], place.along(k)).wait_recv()
    total = got[3]
    for k in range(1, 4):
        total = total + got[3 + k]
    layers = place.layers
    if layers > 1:
        run[4] = total
        got[7 + place.layer] = total
        cps = [
            rcopy(
                run.at[4], got.at[7 + place.layer], send.at[5 + k], recv.at[5 + layers - k],
                place.layer_at(k),
            )
            for k in range(1, layers)
        ]
        for cp in cps:
            cp.start()
        for cp in cps:
            cp.wait_send()
        for k in range(1, layers):
            slot = got.at[7 + lax.rem(place.layer + k, layers)]
            rcopy(slot, slot, send.at[5 + k], recv.at[5 + k], place.layer_at(k)).wait_recv()
        total = got[7]
        for k in range(1, layers):
            total = total + got[7 + k]
    out[...] = total


def input_back(x, gain, grad_in, hg, wq, wk, wv, rhs, dx, vec, windows, pairs):
    tokens = x.shape[0] // windows
    vhat, rstd = normalise(x[...].astype(f32))
    err = jnp.zeros(vhat.shape, f32)
    for part, weight in enumerate((wq, wk, wv)):
        rows = slice(part * HEAD_DIM, (part + 1) * HEAD_DIM)
        for w in range(windows):
            slots = [divmod(w * HEADS + h, pairs) for h in range(HEADS)]
            grad_t = jnp.concatenate([grad_in[s, p, rows, :] for s, p in slots], axis=0)
            rhs[part, w * tokens : (w + 1) * tokens, :] = grad_t.T
        grad = rhs[part]
        err = err + mm_nt(grad, weight[...])
        if part != 1:
            r = 2 + part // 2
            vec[r : r + 1, :] = jnp.sum(grad.astype(f32), axis=0, keepdims=True)
    dv, dgain, dshift = norm_back(err, vhat, rstd, row(gain))
    dx[...] = (hg[...] + dv).astype(bf16)
    vec[0:1, :] = dgain
    vec[1:2, :] = dshift


def backward_kernel(
    dims,
    x, gain1, by_head, bias, mass, do_out, act_t, og, n2_t, pg, bg, hg, att_t, n1_t, vec,
    wq_hbm, wk_hbm, wv_hbm,
    dx, out, vec_out,
    wq, wk, wv, do_in, dqkv_out, dqkv_in, keys_t, v_t, dk, dv, lhs, rhs,
    s_act, s_pg, s_og, s_n2, s_lhs, s_rhs,
    r1, r2, rz, rl, az, run, got,
    load, send, recv, free, do_send, do_recv, dqkv_send, dqkv_recv, core_send, core_recv,
    vec_send, vec_recv,
):
    wins, seqs, windows, pairs = dims
    place = Place(wins, seqs)
    c = place.c
    loads = [
        pltpu.make_async_copy(src, dst, load.at[i])
        for i, (src, dst) in enumerate(((wq_hbm, wq), (wk_hbm, wk), (wv_hbm, wv)))
    ]
    for copy in loads:
        copy.start()
    others = [place.layer_at(k) for k in range(1, place.layers)]
    barrier, expected = place.greet([place.across("a"), place.across("b")])
    pl.semaphore_wait(barrier, expected)

    do_moves = Exchange(place, pairs, do_out, do_in, do_send, do_recv)
    dqkv_moves = Exchange(place, pairs, dqkv_out, dqkv_in, dqkv_send, dqkv_recv)
    for pair in range(pairs):
        do_moves.start(pair)

    core_count = [0]

    def to_core(src, dst):
        i = core_count[0]
        core_count[0] += 1
        cp = rcopy(src, dst, core_send.at[i], core_recv.at[i], place.core())
        cp.start()
        return cp

    theirs = 2 * (1 - c)
    first_moves = [to_core(og, s_og)]
    first_moves += [to_core(act_t.at[theirs + i], s_act.at[i]) for i in range(2)]
    second_moves = [to_core(n2_t, s_n2)]
    second_moves += [to_core(pg.at[theirs + i], s_pg.at[i]) for i in range(2)]
    lhs[0] = n1_t[...]
    lhs[1] = att_t[...]
    rhs[3] = bg[...]
    lhs_moves = [to_core(lhs.at[i], s_lhs.at[i]) for i in range(2)]
    block_ones(keys_t, v_t.shape[1] // BLOCK)

    def fill(index, parts):
        @pl.loop(0, D // 256)
        def _(i):
            rows = span(i * 256, 256)
            (left, right), (left2, right2) = parts
            out[index, rows, :] = (mm(left[rows, :], right[...]) + mm(left2[rows, :], right2[...])).astype(bf16)

    def stream(j):
        index = (j // 2) * 4 + 2 * c + j % 2
        if j < 2:
            parts = ((act_t.at[2 * c + j], og), (s_act.at[j], s_og))
        elif j < 4:
            parts = ((n2_t, pg.at[2 * c + j - 2]), (s_n2, s_pg.at[j - 2]))
        else:
            use_att = c * (j % 2)
            parts = (
                (lhs.at[use_att], rhs.at[2 * c + j % 2]),
                (s_lhs.at[use_att], s_rhs.at[j % 2]),
            )
        fill(index, parts)
        return reduce_halves(place, out, index, j, r1, r2, rz, rl, az, send, recv, free)

    running = []

    def begin(j):
        running.append(stream(j))
        next(running[-1])

    def tick():
        running[:] = [one for one in running if next(one, True) is None]

    for copy in first_moves:
        copy.wait()
    begin(0)
    for copy in second_moves:
        copy.wait()

    def put(tile, pair, value):
        tokens = dqkv_out.shape[-1]
        parts = value.shape[1] // tokens
        for i in range(parts):
            dqkv_out[(tile * parts + i) * pairs + pair, Q_ROWS, :] = value[
                :, i * tokens : (i + 1) * tokens
            ]

    def finish(pair, dk_t, dv_t):
        tokens = dqkv_out.shape[-1]
        for s in range(seqs):
            lanes = slice(s * tokens, (s + 1) * tokens)
            dqkv_out[s * pairs + pair, K_ROWS, :] = dk_t[:, lanes]
            dqkv_out[s * pairs + pair, V_ROWS, :] = dv_t[:, lanes]

    for copy in lhs_moves:
        copy.wait()
    for pair in range(pairs):
        do_moves.arrived(pair)
        tick()
        if pair + 1 < 4:
            begin(pair + 1)
        attend_pair_back(
            pair, by_head, do_in, bias, mass, keys_t, v_t, dk, dv, put, finish
        )
        dqkv_moves.start(pair)
    for j in range(pairs + 1, 4):
        tick()
        begin(j)
    tick()
    for pair in range(pairs):
        dqkv_moves.arrived(pair)
    for copy in loads:
        copy.wait()
    run[0] = vec[...]
    input_back(x, gain1, dqkv_in, hg, wq, wk, wv, rhs, dx, run.at[0], windows, pairs)
    rhs_moves = [to_core(rhs.at[theirs + i], s_rhs.at[i]) for i in range(2)]
    running.append(reduce_vectors(place, vec_out, run, got, vec_send, vec_recv))
    next(running[-1])
    tick()
    for copy in rhs_moves:
        copy.wait()
    begin(4)
    tick()
    begin(5)
    while running:
        tick()
    for pair in range(pairs):
        do_moves.sent(pair)
        dqkv_moves.sent(pair)


def bias_rows(random_blocks, blocks, windows_of, rows):
    query = jnp.arange(blocks)[None, :]
    key = jnp.arange(blocks)[:, None]
    fixed = (
        ((key == query - 1) & (query > 0)).astype(f32)
        + (key == query)
        + ((key == query + 1) & (query < blocks - 1))
        + (key == 0)
        + (key == blocks - 1)
    )
    mine = windows_of[:, None, None, None] == jnp.arange(random_blocks.shape[0])[None, :, None, None]
    chosen = jnp.sum(jnp.where(mine, random_blocks[None], 0), axis=1)
    picks = jnp.sum(chosen[:, None, :, :] == key[None, :, :, None], axis=3)
    count = fixed[None] + picks.astype(f32)
    rest = jnp.where(count > 0, jnp.log(jnp.maximum(count, 1.0)), masked_score)
    terms = []
    for _ in range(3):
        terms.append(lax.reduce_precision(rest, 8, 7))
        rest = jnp.where(count > 0, rest - terms[-1], 0.0)
    table = jnp.concatenate(terms, axis=1)
    table = jnp.pad(table, ((0, 0), (0, rows - 3 * blocks), (0, 0)))
    return jnp.repeat(table.astype(bf16), BLOCK, axis=2)


def body(
    tokens,
    cotangent,
    group_ids,
    random_blocks,
    norm1_gain,
    norm1_bias,
    query_weight,
    query_bias,
    key_weight,
    value_weight,
    value_bias,
    out_weight,
    out_bias,
    norm2_gain,
    norm2_bias,
    up_weight,
    up_bias,
    down_weight,
    down_bias,
):
    seqs, wins = lax.axis_size("seq"), lax.axis_size("win")
    windows, here, _ = tokens.shape
    length = here * seqs
    blocks = length // BLOCK
    rows = windows * here
    pairs = -(-windows * HEADS // seqs)
    slots = pairs * seqs
    layers = seqs // 8
    extra = -(-(HEAD_DIM + 3 * blocks) // 128) * 128 - HEAD_DIM
    dims = (wins, seqs, windows, pairs)
    struct = jax.ShapeDtypeStruct
    dma = pltpu.SemaphoreType.DMA
    vmem = pltpu.VMEM

    first = lax.axis_index("seq") * pairs
    windows_of = jnp.minimum((first + jnp.arange(pairs)) // HEADS, windows - 1)
    bias = bias_rows(random_blocks, blocks, windows_of, extra)
    x = tokens.reshape(rows, D)

    y, by_head, mass, act_t, og, n2_t, pg, bg, hg, do_out, att_t, n1_t, vec = pl.pallas_call(
        functools.partial(forward_kernel, dims),
        out_shape=(
            struct((rows, D), bf16),
            struct((seqs, pairs, 3 * HEAD_DIM, here), bf16),
            struct((pairs, 1, length), f32),
            struct((TILES, D, rows), bf16),
            struct((rows, D), bf16),
            struct((D, rows), bf16),
            struct((TILES, rows, D), bf16),
            struct((rows, D), bf16),
            struct((rows, D), f32),
            struct((slots, HEAD_DIM, here), bf16),
            struct((D, rows), bf16),
            struct((D, rows), bf16),
            struct((VEC_ROWS, D), f32),
        ),
        in_specs=[in_smem]
        + [in_vmem] * 9
        + [anywhere, anywhere]
        + [in_vmem] * 3
        + [anywhere, in_vmem, anywhere, in_vmem],
        out_specs=(in_vmem,) * 13,
        scratch_shapes=[
            vmem((slots, 3 * HEAD_DIM, here), bf16),
            vmem((slots, HEAD_DIM, here), bf16),
            vmem((seqs, pairs, HEAD_DIM, here), bf16),
            vmem((HEAD_DIM + extra, length), bf16),
            vmem((HEAD_DIM, length), bf16),
            vmem((wins, 8, 128), f32),
            vmem((rows, D), bf16),
            vmem((D, D), bf16),
            vmem((D, FF), bf16),
            vmem((FF, D), bf16),
            dma((4,)),
            dma((seqs, pairs)),
            dma((seqs, pairs)),
            dma((seqs, pairs)),
            dma((seqs, pairs)),
            dma((wins,)),
            dma((wins,)),
        ],
        compiler_params=pltpu.CompilerParams(
            collective_id=0, has_side_effects=True, vmem_limit_bytes=VMEM_LIMIT
        ),
    )(
        group_ids, x, norm1_gain, norm1_bias, query_weight, query_bias, key_weight, value_weight,
        value_bias, bias, cotangent.reshape(rows, D), out_weight, out_bias, norm2_gain, norm2_bias,
        up_weight, up_bias, down_weight, down_bias,
    )

    layer_slots = layers if layers > 1 else 1
    halves = 2 * OWN
    dx, sums, vec_sums = pl.pallas_call(
        functools.partial(backward_kernel, dims),
        out_shape=(
            struct((rows, D), bf16),
            struct((2 * OWN, D, D), bf16),
            struct((VEC_ROWS, D), f32),
        ),
        in_specs=[in_vmem] * 15 + [anywhere] * 3,
        out_specs=(in_vmem,) * 3,
        scratch_shapes=[
            vmem((D, D), bf16),
            vmem((D, D), bf16),
            vmem((D, D), bf16),
            vmem((seqs, pairs, HEAD_DIM, here), bf16),
            vmem((slots, 3 * HEAD_DIM, here), bf16),
            vmem((seqs, pairs, 3 * HEAD_DIM, here), bf16),
            vmem((HEAD_DIM + extra, length), bf16),
            vmem((HEAD_DIM, length), bf16),
            vmem((length, HEAD_DIM), f32),
            vmem((length, HEAD_DIM), f32),
            vmem((2, D, rows), bf16),
            vmem((4, rows, D), bf16),
            vmem((2, D, rows), bf16),
            vmem((2, rows, D), bf16),
            vmem((rows, D), bf16),
            vmem((D, rows), bf16),
            vmem((2, D, rows), bf16),
            vmem((2, rows, D), bf16),
            vmem((halves, D // 2, HALF), bf16),
            vmem((halves, D // 4, HALF), bf16),
            vmem((halves, 3, D // 16, HALF), bf16),
            vmem((halves, layer_slots, D // 16, HALF), bf16),
            vmem((halves, 3, D // 16, HALF), bf16),
            vmem((5, VEC_ROWS, D), f32),
            vmem((7 + layers, VEC_ROWS, D), f32),
            dma((3,)),
            dma((halves, 11 + layers)),
            dma((halves, 11 + layers)),
            pltpu.SemaphoreType.REGULAR((halves, 2)),
            dma((seqs, pairs)),
            dma((seqs, pairs)),
            dma((seqs, pairs)),
            dma((seqs, pairs)),
            dma((10,)),
            dma((10,)),
            dma((6 + layers,)),
            dma((6 + layers,)),
        ],
        compiler_params=pltpu.CompilerParams(
            collective_id=1, has_side_effects=True, vmem_limit_bytes=VMEM_LIMIT
        ),
    )(
        x, norm1_gain, by_head, bias, mass, do_out, act_t, og, n2_t, pg, bg, hg, att_t, n1_t, vec,
        query_weight, key_weight, value_weight,
    )

    down_grad = sums[0:4].reshape(FF, D).astype(f32)
    up_grad = jnp.transpose(sums[4:8].astype(f32), (1, 0, 2)).reshape(D, FF)
    query_grad, key_grad, value_grad, out_grad = (sums[8 + i].astype(f32) for i in range(4))
    return (
        y.reshape(tokens.shape),
        dx.reshape(tokens.shape),
        vec_sums[0],
        vec_sums[1],
        query_grad,
        vec_sums[2],
        key_grad,
        value_grad,
        vec_sums[3],
        out_grad,
        vec_sums[4],
        vec_sums[5],
        vec_sums[6],
        up_grad,
        vec_sums[8:12].reshape(FF),
        down_grad,
        vec_sums[7],
    )


def solution(mesh):
    split = P("win", "seq", None)
    return jax.shard_map(
        body,
        mesh=mesh,
        in_specs=(split, split, P("win"), P("win", None, None)) + (P(),) * 15,
        out_specs=(split, split) + (P(),) * 15,
        check_vma=False,
    )
```

time: 392 us -> 274 us (0.70)
  waiting for transfers between devices: 57.9 us -> 0 us
  blocking collectives: 27.6 us -> 0 us
  Pallas kernels: 246 us -> 225 us
  starting transfers between devices: 13.3 us -> 0 us
  other arithmetic: 16.1 us -> 20.6 us
    all_to_all x3 -> x0, waiting for transfers between devices: 57.9 us -> none  [exchange(): return lax.all_to_all(v, 'seq', split_axis=0, concat_axis=0, tiled=True)]
    pallas_call x6 -> x2, Pallas kernels: 246 us -> 225 us  [the longest x1 168 us: body(): pl.pallas_call(functools.partial(backward_kernel, dims), out_shape=(struc...]
    all_to_all x1 -> x0, blocking collectives: 17.7 us -> none  [exchange(): return lax.all_to_all(v, 'seq', split_axis=0, concat_axis=0, tiled=True)]
    all_to_all x3 -> x0, starting transfers between devices: 13.3 us -> none  [exchange(): return lax.all_to_all(v, 'seq', split_axis=0, concat_axis=0, tiled=True)]
    psum x1 -> x0, blocking collectives: 9.89 us -> none  [body(): group_sizes = lax.psum(jnp.sum(membership, axis=0), 'win')]
    unnamed x24 -> x8, local copies, waits for them, and re-layouts: 1.88 us -> 11.3 us
    slice x3 -> x0, local copies, waits for them, and re-layouts: 8.86 us -> none  [the longest x1 8.12 us: body(): down_grad = sums[0:2].reshape(FF, D).astype(f32)]
    slice x0 -> x1, other arithmetic: none -> 8.59 us  [body(): down_grad = sums[0:4].reshape(FF, D).astype(f32)]
  transfers between devices with their start and end apart: 3 -> 0, of which waited for: 2 -> 0; matrix products, arithmetic and copies ran while one was open for 1% -> 0% of each run, Pallas kernels for 0% -> 0%
where the time goes in v2:
time: 274 us; the launch traced here: 272 us
  Pallas kernels  225 us (82%)
  local copies, waits for them, and re-layouts  26.2 us (10%)
  other arithmetic  20.6 us (8%)
    pallas_call x1, Pallas kernels, body(): pl.pallas_call(functools.partial(backward_kernel, dims), out_shape=(struc...  168 us
    pallas_call x1, Pallas kernels, body(): pl.pallas_call(functools.partial(forward_kernel, dims), out_shape=(struct...  56.2 us
    unnamed x8, local copies, waits for them, and re-layouts  11.3 us
    reshape x1, local copies, waits for them, and re-layouts, body(): up_grad = jnp.transpose(sums[4:8].astype(f32), (1, 0, 2)).reshape(D, FF)  9.66 us
    slice x1, other arithmetic, body(): down_grad = sums[0:4].reshape(FF, D).astype(f32)  8.59 us
    convert_element_type x1, other arithmetic, body(): sums[8 + i].astype(f32)  6.18 us

profile of v2, /device:TPU:0, one launch (start us, length us, event | category | flops | bytes accessed | tf_op | source)
XLA Modules:
  0.0 272.2 jit_solution(13062130328431823898)
XLA Ops:
  0.7 0.1 iota_compare_fusion.4
  0.8 0.1 add_add_fusion
  0.8 0.8 select_reduce_fusion
  1.7 0.1 copy.44
  1.8 0.1 copy.45
  1.8 0.1 copy.46
  1.9 0.1 pad_maximum_fusion
  2.0 0.1 copy.50
  2.1 0.5 broadcast_in_dim.40
  2.6 1.3 reshape.256.bias
  3.9 56.2 %shard_map.314 = (bf16[256,768]{1,0:T(8,128)(2,1)}, bf16[8,3,192,128]{3,2,1,0:T(8,128)(2,1)}, f32[3,1,1024]{2,1,0:T(1,128)}, bf16[4,768,256]{2,1,0:T(8,128)(2,1)...) custom-call(s32[2]{0:T(128)} %ids.1, ...), custom_call_target="tpu_custom_call" | custom-call | tf_op jit(solution)/shard_map/pallas_call | solution.py:785
  60.1 168.5 %shard_map.315 = (bf16[256,768]{1,0:T(8,128)(2,1)}, bf16[12,768,768]{2,1,0:T(8,128)(2,1)}, f32[16,768]{1,0:T(8,128)}) custom-call(bf16[256,768]{1,0:T(8,128)(2,1)} %bitcast.26, f32[768]{0:T(1024)} %gain1.3, bf16[8,3,192,128]{3,2,1,0:T(8,128)(2,1)} %get-tuple-element.34.by_head, bf16[3,64,1024]{2,1,0:T(8,128)(2,1)} %reshape.256.bias, ...), custom_call_target="tpu_custom_call" | custom-call | tf_op jit(solution)/shard_map/pallas_call | solution.py:838
  228.6 0.7 slice.57
  229.4 1.9 slice_reduce_fusion
  231.3 0.6 reshape.262
  231.9 6.2 %bitcast_convert_fusion.1 = (f32[768,768]{1,0:T(8,128)}, f32[768,768]{1,0:T(8,128)}, f32[768,768]{1,0:T(8,128)}, f32[768,768]{1,0:T(8,128)}) fusion(bf16[12,768,768]{2,1,0:T(8,128)(2,1)} %get-tuple-element.48), kind=kLoop, calls=%fused_computation.2 | loop fusion | flops 2359296 | bytes 14155776 | tf_op jit(solution)/shard_map/convert_element_type | solution.py:896
  238.0 8.6 %fusion.8 = (bf16[4,768,768]{2,1,0:T(8,128)(2,1)S(1)}, f32[768,4,768]{2,0,1:T(8,128)}) fusion(bf16[12,768,768]{2,1,0:T(8,128)(2,1)} %get-tuple-element.48), kind=kLoop, calls=%fused_computation.44 | loop fusion | flops 2359296 | bytes 23592960 | tf_op jit(solution)/shard_map/slice | solution.py:894
  246.6 4.8 %bitcast_convert_fusion = f32[3072,768]{1,0:T(8,128)} fusion(bf16[4,768,768]{2,1,0:T(8,128)(2,1)S(1)} %get-tuple-element.108), kind=kLoop, calls=%fused_computation.1 | loop fusion | flops 2359296 | bytes 14155776 | tf_op jit(solution)/shard_map/convert_element_type | solution.py:894
  251.4 9.7 %copy.48 = f32[768,4,768]{0,2,1:T(8,128)} copy(f32[768,4,768]{2,0,1:T(8,128)} %get-tuple-element.109) | data formatting | bytes 18874368 | tf_op jit(solution)/shard_map/reshape | solution.py:895
  261.1 0.0 copy-start
  261.1 0.0 copy-start.1
  261.1 9.7 %copy.49 = f32[768,3072]{1,0:T(8,128)} copy(f32[768,3072]{0,1:T(8,128)} %bitcast.24) | data formatting | bytes 18874368
  270.7 0.0 copy-done
  270.7 0.7 copy.53
  271.5 0.0 copy-done.1
  271.5 0.7 copy.54
  (7 shorter events, 0.1 us)
Async XLA Ops:
  261.1 9.7 %copy-start = (bf16[256,768]{1,0:T(8,128)(2,1)S(1)}, bf16[256,768]{1,0:T(8,128)(2,1)}, u32[]{:S(2)}) copy-start(bf16[256,768]{1,0:T(8,128)(2,1)} %get-tuple-element.33) | copy-start | bytes 1179652
  261.1 10.4 %copy-start.1 = (bf16[256,768]{1,0:T(8,128)(2,1)S(1)}, bf16[256,768]{1,0:T(8,128)(2,1)}, u32[]{:S(2)}) copy-start(bf16[256,768]{1,0:T(8,128)(2,1)} %get-tuple-element.46) | copy-start | bytes 1179652

commit v3 on v0

v3 whole, which is shorter than its diff:
```python
import functools
import math

import jax
import jax.numpy as jnp
from jax import lax
from jax.experimental import pallas as pl
from jax.experimental.pallas import tpu as pltpu
from jax.sharding import PartitionSpec as P

D = 768
HEADS = 12
HEAD_DIM = 64
FF = 3072
BLOCK = 64
RAND = 3
GROUPS = 8
TILES = FF // D
VEC_ROWS = 16
OWN = 6
HALF = D // 2
VECTORS = 12
ORDERS = (
    "labh", "balh", "ablh", "balh",
    "ablh", "balh", "ablh", "blah",
    "ablh", "balh", "ablh", "balh",
)
SCHEDULE = (
    "2301AAA23504123765Wv01234vX9876v45ab0v79",
    "184v25630v1a647vb215983026b49a71853260b4",
    "93a178541162722530b963a380047b4594a8655b",
    "a9676b877a898899abaabb",
)

MESH = pl.DeviceIdType.MESH
VMEM_LIMIT = 63 << 20
epsilon = 1e-05
masked_score = -1e30
score_scale = HEAD_DIM ** (-0.5)
f32 = jnp.float32
bf16 = jnp.bfloat16

in_vmem = pl.BlockSpec(memory_space=pltpu.VMEM)
in_smem = pl.BlockSpec(memory_space=pltpu.SMEM)
anywhere = pl.BlockSpec(memory_space=pl.ANY)


def mm(left, right):
    return jnp.dot(left, right, preferred_element_type=f32)


def mm_nt(left, right):
    return lax.dot_general(left, right, (((1,), (1,)), ((), ())), preferred_element_type=f32)


def row(ref):
    return ref[...].reshape(1, -1)


def normalise(v):
    centre = v - jnp.mean(v, axis=-1, keepdims=True)
    rstd = lax.rsqrt(jnp.mean(centre * centre, axis=-1, keepdims=True) + epsilon)
    return centre * rstd, rstd


def norm_back(err, vhat, rstd, gain):
    g = err * gain
    dv = rstd * (
        g - jnp.mean(g, axis=-1, keepdims=True) - vhat * jnp.mean(g * vhat, axis=-1, keepdims=True)
    )
    return dv, jnp.sum(err * vhat, axis=0, keepdims=True), jnp.sum(err, axis=0, keepdims=True)


def rcopy(src, dst, send, recv, device):
    return pltpu.make_async_remote_copy(
        src, dst, send, recv, device_id=device, device_id_type=MESH
    )


def span(start, size):
    return pl.ds(pl.multiple_of(start, 16), size)


class Place:
    def __init__(self, wins, seqs):
        self.wins, self.seqs = wins, seqs
        self.layers = seqs // 8
        self.w = lax.axis_index("win")
        self.s = lax.axis_index("seq")
        self.c = lax.rem(self.s, 2)
        self.z = lax.rem(self.s // 2, 4)
        self.layer = self.s // 8
        self.layer_steps = (seqs // 8).bit_length() - 1
        self.size = seqs // 2
        self.window = self.s // self.size
        self.g = lax.rem(self.s, self.size)
        self.base = self.s - self.g
        self.core_free = None
        self.bits = {"a": lax.rem(self.w, 2), "b": self.w // 2}

    def core(self):
        return (self.w, self.s + 1 - 2 * self.c)

    def across(self, axis):
        step = 1 if axis == "a" else 2
        return (self.w + step - 2 * step * self.bits[axis], self.s)

    def along(self, k):
        return (self.w, self.layer * 8 + lax.rem(self.z + k, 4) * 2 + self.c)

    def layer_swap(self, i):
        step = 2**i
        bit = lax.rem(self.layer // step, 2)
        return (self.w, self.s + 8 * step * (1 - 2 * bit))

    def step_z(self, step):
        bit = lax.rem(self.z // step, 2)
        return (self.w, self.s + 2 * step * (1 - 2 * bit))

    def core_open(self):
        if self.core_free is not None:
            pl.semaphore_wait(self.core_free, 1)
            self.core_free = None

    def group_at(self, k):
        return (self.w, self.base + lax.rem(self.g + k, self.size))

    def partner(self):
        return (self.w, lax.rem(self.s + self.size, self.seqs))

    def win_at(self, k):
        return (lax.rem(self.w + k, self.wins), self.s)

    def greet(self):
        barrier = pltpu.get_barrier_semaphore()

        def one(k, carry):
            pl.semaphore_signal(barrier, inc=1, device_id=self.group_at(k), device_id_type=MESH)
            return carry

        lax.fori_loop(1, self.size, one, 0)
        others = [self.partner()]
        others += [self.win_at(k) for k in range(1, self.wins)]
        others += [self.layer_swap(i) for i in range(self.layer_steps)]
        for peer in others:
            pl.semaphore_signal(barrier, inc=1, device_id=peer, device_id_type=MESH)
        pl.semaphore_wait(barrier, self.size - 1 + len(others))


class Exchange:
    def __init__(self, place, pairs, out, into, send, recv):
        self.place, self.pairs = place, pairs
        self.out, self.into, self.send, self.recv = out, into, send, recv

    def copy(self, k, pair, part, lanes):
        place = self.place
        target = lax.rem(place.g + k, place.size)
        return rcopy(
            self.out.at[target * self.pairs + pair, :, lanes],
            self.into.at[place.g, pair, :, lanes],
            self.send.at[k, pair, part],
            self.recv.at[k, pair, part],
            place.group_at(k),
        )

    def start(self, pair, part=0, lanes=slice(None)):
        def one(k, carry):
            self.copy(k, pair, part, lanes).start()
            return carry

        place = self.place
        lax.fori_loop(1, place.size, one, 0)
        self.into[place.g, pair, :, lanes] = self.out[place.g * self.pairs + pair, :, lanes]

    def arrived(self, pair, part=0, lanes=slice(None)):
        def one(k, carry):
            place = self.place
            slot = self.into.at[lax.rem(place.g + place.size - k, place.size), pair, :, lanes]
            rcopy(
                slot, slot, self.send.at[k, pair, part], self.recv.at[k, pair, part],
                place.group_at(k),
            ).wait_recv()
            return carry

        lax.fori_loop(1, self.place.size, one, 0)

    def sent(self, pair, part=0, lanes=slice(None)):
        def one(k, carry):
            self.copy(k, pair, part, lanes).wait_send()
            return carry

        lax.fori_loop(1, self.place.size, one, 0)


Q_ROWS, K_ROWS, V_ROWS = (slice(i * HEAD_DIM, (i + 1) * HEAD_DIM) for i in range(3))


def tile_width(length):
    return 256 if length <= 2048 else 128


def block_at(place, first, shape, axis):
    index = first + lax.broadcasted_iota(jnp.int32, shape, axis)
    slot, half = index // 256, lax.rem(index // 128, 2)
    window = place.window + half - 2 * half * place.window
    return (window * place.size + slot) * 2 + lax.rem(index // BLOCK, 2)


def block_ones(place, keys, blocks):
    length, lanes = keys.shape

    def one_group(group, carry):
        shape = (256, lanes)
        part = lax.broadcasted_iota(jnp.int32, shape, 1) - HEAD_DIM
        block = block_at(place, group * 256, shape, 0)
        hit = (part == block) | (part == block + blocks) | (part == block + 2 * blocks)
        keys[span(group * 256, 256), :] = jnp.where(hit, 1.0, 0.0).astype(bf16)
        return carry

    lax.fori_loop(0, length // 256, one_group, 0)


def gather_rows(ref, pair, rows, into):
    tokens = ref.shape[3]
    for s in range(ref.shape[0]):
        into[: rows.stop - rows.start, s * tokens : (s + 1) * tokens] = ref[s, pair, rows, :]


def place_of_tile(tile, width):
    per_slot = 256 // width
    if per_slot == 1:
        return tile, slice(None)
    return tile // per_slot, pl.ds(pl.multiple_of(lax.rem(tile, per_slot) * width, width), width)


def biased_scores(keys, q_t, bias, lanes):
    return mm(keys[...], jnp.concatenate([q_t, bias[:, lanes]], axis=0))


def attend_pair(pair, qkv, bias, keys, k_t, v_t, small_out, raw, mass):
    length = v_t.shape[1]
    pairs = qkv.shape[1]
    width = tile_width(length)
    step = length if length <= 1024 else 512
    gather_rows(qkv, pair, K_ROWS, k_t)
    gather_rows(qkv, pair, V_ROWS, v_t)
    keys[:, :HEAD_DIM] = k_t[...].T

    def one_tile(tile, carry):
        lanes = pl.ds(pl.multiple_of(tile * width, width), width)
        slot, within = place_of_tile(tile, width)
        q_t = qkv[slot, pair, Q_ROWS, within]
        parts = [slice(first, first + step) for first in range(0, length, step)]
        scores = [biased_scores(keys.at[part], q_t, bias, lanes) for part in parts]
        top = jnp.max(scores[0], axis=0, keepdims=True)
        for more in scores[1:]:
            top = jnp.maximum(top, jnp.max(more, axis=0, keepdims=True))
        total, got = 0.0, 0.0
        for i, part in enumerate(parts):
            held = scores[0] if len(parts) == 1 else biased_scores(keys.at[part], q_t, bias, lanes)
            weight = jnp.exp(held - top)
            total = total + jnp.sum(weight, axis=0, keepdims=True)
            got = got + mm(v_t[:, part], weight.astype(bf16))
        mass[pair, :, lanes] = top + jnp.log(total)
        got = got * (1.0 / total)
        raw[pair, :, lanes] = got
        small_out[slot * pairs + pair, :, within] = got.astype(bf16)
        return carry

    lax.fori_loop(0, length // width, one_tile, 0)


def attend_pair_back(pair, qkv, grad, bias, raw, mass, keys, k_t, v_t, dk, dv, out):
    length = v_t.shape[1]
    pairs = qkv.shape[1]
    width = tile_width(length)
    step = length if length <= 1024 else 512
    gather_rows(qkv, pair, K_ROWS, k_t)
    gather_rows(qkv, pair, V_ROWS, v_t)
    keys[:, :HEAD_DIM] = k_t[...].T
    values = v_t[...].T
    dk[...] = jnp.zeros_like(dk)
    dv[...] = jnp.zeros_like(dv)

    def one_tile(tile, carry):
        lanes = pl.ds(pl.multiple_of(tile * width, width), width)
        slot, within = place_of_tile(tile, width)
        q_t = qkv[slot, pair, Q_ROWS, within]
        g_t = grad[slot, pair, :, within]
        row_dot = jnp.sum(g_t.astype(f32) * raw[pair, :, lanes], axis=0, keepdims=True)
        dq = jnp.zeros(q_t.shape, f32)
        for first in range(0, length, step):
            part = slice(first, first + step)
            probs = jnp.exp(biased_scores(keys.at[part], q_t, bias, lanes) - mass[pair, :, lanes])
            score_grad = (probs * (mm(values[part], g_t) - row_dot)).astype(bf16)
            dq = dq + mm(k_t[:, part], score_grad)
            dk[:, part] += mm_nt(q_t, score_grad)
            dv[:, part] += mm_nt(g_t, probs.astype(bf16))
        out[slot * pairs + pair, Q_ROWS, within] = (dq * score_scale).astype(bf16)
        return carry

    lax.fori_loop(0, length // width, one_tile, 0)
    dk_t, dv_t = dk[...].astype(bf16), dv[...].astype(bf16)
    for slot in range(qkv.shape[0]):
        lanes = slice(slot * 256, (slot + 1) * 256)
        out[slot * pairs + pair, K_ROWS, :] = dk_t[:, lanes]
        out[slot * pairs + pair, V_ROWS, :] = dv_t[:, lanes]


def project_qkv(half, xs, gain, shift, weights, biases, out, n1_t, wait):
    tokens = xs.shape[0] // 2
    here = slice(half * tokens, (half + 1) * tokens)
    vhat, _ = normalise(xs[here, :].astype(f32))
    n1 = (vhat * row(gain) + row(shift)).astype(bf16)
    n1_t[:, here] = n1.T
    for part in range(3):
        wait(part)
        y = mm(n1, weights[part])
        if biases[part] is not None:
            y = y + row(biases[part])
        y = y.astype(bf16)
        if part == 0:
            y = y * jnp.asarray(score_scale, bf16)
        y_t = y.T
        for h in range(HEADS):
            out[h, part * HEAD_DIM : (part + 1) * HEAD_DIM, here] = y_t[
                h * HEAD_DIM : (h + 1) * HEAD_DIM, :
            ]


def fill_bias(place, picks, bias, blocks):
    rows, length = bias.shape
    bias[...] = jnp.zeros_like(bias)

    def one_group(group, carry):
        lanes = pl.ds(pl.multiple_of(group * 128, 128), 128)
        key = lax.broadcasted_iota(jnp.int32, (blocks, 128), 0)
        query = block_at(place, group * 128, (blocks, 128), 1)
        count = (
            jnp.where((key == query - 1) & (query > 0), 1.0, 0.0)
            + jnp.where(key == query, 1.0, 0.0)
            + jnp.where((key == query + 1) & (query < blocks - 1), 1.0, 0.0)
            + jnp.where(key == 0, 1.0, 0.0)
            + jnp.where(key == blocks - 1, 1.0, 0.0)
        )
        half = lax.rem(group, 2)
        window = place.window + half - 2 * half * place.window
        first = (window * place.size + group // 2) * 2
        for side in range(2):
            for r in range(RAND):
                pick = picks[place.window, first + side, r]
                count = count + jnp.where((key == pick) & (query == first + side), 1.0, 0.0)
        listed = count > 0.0
        rest = jnp.where(listed, jnp.log(jnp.maximum(count, 1.0)), masked_score)
        for term in range(3):
            part = rest.astype(bf16)
            bias[term * blocks : (term + 1) * blocks, lanes] = part
            rest = jnp.where(listed, rest - part.astype(f32), 0.0)
        return carry

    lax.fori_loop(0, length // 128, one_group, 0)


def input_back(xs, gain, grad_in, hg, weights, rhs, vec):
    pairs = grad_in.shape[1]
    vhat, rstd = normalise(xs[...].astype(f32))
    err = jnp.zeros(vhat.shape, f32)
    slots = [divmod(h, pairs) for h in range(HEADS)]
    for part in range(3):
        rows = slice(part * HEAD_DIM, (part + 1) * HEAD_DIM)
        rhs[part] = jnp.concatenate([grad_in[s, p, rows, :] for s, p in slots], axis=0).T
        grad = rhs[part]
        err = err + mm_nt(grad, weights[part])
        if part != 1:
            r = 2 + part // 2
            vec[r : r + 1, :] = jnp.sum(grad.astype(f32), axis=0, keepdims=True)
    dv, dgain, dshift = norm_back(err, vhat, rstd, row(gain))
    vec[0:1, :] = dgain
    vec[1:2, :] = dshift
    return (hg[...] + dv).astype(bf16)


def reduce_piece(place, order, out, out_hbm, store, mine, other, bufs, rl, send, recv, free):
    index, col = mine
    cols = pl.ds(col, HALF)
    buf = out.at[index]
    ways = {
        "a": (place.bits["a"], place.across("a")),
        "b": (place.bits["b"], place.across("b")),
        "l": (lax.rem(place.z, 2), place.step_z(1)),
        "h": (place.z // 2, place.step_z(2)),
    }
    hops = [ways[axis] for axis in order]

    def at(start, size):
        return buf.at[span(start, size), cols]

    start, size = 0, D
    spans = []
    for i, (bit, partner) in enumerate(hops):
        size = size // 2
        keep, away = start + bit * size, start + (1 - bit) * size
        if i:
            source = bufs[i - 1]
            at(away, size)[...] = at(away, size)[...] + source[span((1 - bit) * size, size)]
        cp = rcopy(at(away, size), bufs[i], send.at[i], recv.at[i], partner)
        cp.start()
        if i:
            at(keep, size)[...] = at(keep, size)[...] + source[span(bit * size, size)]
        start = keep
        spans.append((keep, size))
        yield
        cp.wait()
        pl.semaphore_signal(free.at[i], inc=1, device_id=partner, device_id_type=MESH)
    held = at(start, size)
    held[...] = held[...] + bufs[-1][...]
    for i in range(place.layer_steps):
        cp = rcopy(held, rl.at[i], send.at[9 + i], recv.at[9 + i], place.layer_swap(i))
        cp.start()
        cp.wait()
        held[...] = held[...] + rl[i]
    for i in reversed(range(len(hops))):
        pl.semaphore_wait(free.at[i], 1)
        held = at(*spans[i])
        cp = rcopy(held, held, send.at[4 + i], recv.at[4 + i], hops[i][1])
        cp.start()
        yield
        cp.wait()
    place.core_open()
    held = buf.at[:, cols]
    cp = rcopy(held, held, send.at[8], recv.at[8], place.core())
    cp.start()
    yield
    cp.wait()
    copies = []
    for i, (block, column) in enumerate((mine, other)):
        where = (block, slice(None), pl.ds(column, HALF))
        copies.append(pltpu.make_async_copy(out.at[where], out_hbm.at[where], store.at[i]))
        copies[-1].start()
    yield
    for copy in copies:
        copy.wait()


def reduce_vectors(place, out, run, got, send, recv):
    for step, device in enumerate((place.core(), place.across("a"), place.across("b"))):
        cp = rcopy(run.at[step], got.at[step], send.at[step], recv.at[step], device)
        cp.start()
        yield
        cp.wait()
        run[step + 1] = run[step] + got[step]
    got[3 + place.z] = run[3]
    cps = [
        rcopy(run.at[3], got.at[3 + place.z], send.at[2 + k], recv.at[6 - k], place.along(k))
        for k in (1, 2, 3)
    ]
    for cp in cps:
        cp.start()
    yield
    for cp in cps:
        cp.wait_send()
    for k in (1, 2, 3):
        slot = got.at[3 + lax.rem(place.z + k, 4)]
        rcopy(slot, slot, send.at[2 + k], recv.at[2 + k], place.along(k)).wait_recv()
    total = got[3]
    for k in range(1, 4):
        total = total + got[3 + k]
    for i in range(place.layer_steps):
        run[4] = total
        cp = rcopy(run.at[4], got.at[7 + i], send.at[6 + i], recv.at[6 + i], place.layer_swap(i))
        cp.start()
        cp.wait()
        total = total + got[7 + i]
    out[...] = total


def layer_kernel(
    dims,
    ids, x, gain1, shift1, bq, bv, bo, gain2, shift2, bup, bdown,
    picks_hbm, cot_hbm, wq_hbm, wk_hbm, wv_hbm, wo_hbm, wup_hbm, wdown_hbm,
    y, dx, vec_out, out_hbm,
    picks, out, xs, y_sent, y_got, wqkv, wo, og, lhs, rhs, n2_t, act_t, pg, hg, dact, up_bias,
    s_og, s_n2, s_act, s_pg, s_lhs, s_rhs,
    head_out, by_head, small_out, att_in, do_in, dqkv_in, bias, raw, mass, keys, k_t, v_t, counts,
    r0, r1, r2, r3, rl, run, got,
    load, store, piece_send, piece_recv, free, core_free, core_send, core_recv,
    qkv_send, qkv_recv, att_send, att_recv, do_send, do_recv, dqkv_send, dqkv_recv,
    count_send, count_recv, vec_send, vec_recv, swap_send, swap_recv,
):
    wins, seqs, windows, pairs = dims
    place = Place(wins, seqs)
    c = place.c
    tokens = x.shape[0] // windows
    kept = pl.ds(pl.multiple_of(place.window * tokens, tokens), tokens)
    moved = pl.ds(pl.multiple_of((1 - place.window) * tokens, tokens), tokens)
    lower, upper = slice(0, tokens), slice(tokens, 2 * tokens)
    length = v_t.shape[1]
    blocks = length // BLOCK
    theirs, ours = 2 * (1 - c), 2 * c

    def up_tile(t):
        return out.at[(t // 2) * 4 + theirs + lax.rem(t, 2)]

    def down_tile(t):
        return out.at[8 + t]

    moves = [(wq_hbm, wqkv.at[0]), (wk_hbm, wqkv.at[1]), (wv_hbm, wqkv.at[2])]
    moves += [(cot_hbm.at[kept], og.at[lower])]
    moves += [(wdown_hbm.at[t * D : (t + 1) * D], down_tile(t)) for t in range(TILES)]
    moves += [(wo_hbm, wo), (picks_hbm, picks)]
    moves += [(wup_hbm.at[:, t * D : (t + 1) * D], up_tile(t)) for t in range(TILES)]
    loads = [pltpu.make_async_copy(src, dst, load.at[i]) for i, (src, dst) in enumerate(moves)]
    for copy in loads:
        copy.start()
    place.greet()

    def swap(i, src, dst):
        copy = rcopy(src, dst, swap_send.at[i], swap_recv.at[i], place.partner())
        copy.start()
        return copy

    x_swap = swap(0, x.at[moved], xs.at[upper])
    lane = lax.broadcasted_iota(jnp.int32, (8, 128), 1)
    member = [jnp.where(lane == ids[w], 1.0, 0.0) for w in range(windows)]
    counts[place.w] = sum(member[1:], member[0])
    mine = counts.at[place.w]
    count_moves = [
        rcopy(mine, mine, count_send.at[k], count_recv.at[k], place.win_at(k))
        for k in range(1, wins)
    ]
    for copy in count_moves:
        copy.start()
    for t in range(TILES):
        up_bias[t : t + 1, :] = bup[t * D : (t + 1) * D].reshape(1, D)
    for p in range(HEADS, head_out.shape[0]):
        head_out[p] = jnp.zeros(head_out.shape[1:], bf16)

    qkv_moves = Exchange(place, pairs, head_out, by_head, qkv_send, qkv_recv)
    att_moves = Exchange(place, pairs, small_out, att_in, att_send, att_recv)
    do_moves = Exchange(place, pairs, small_out, do_in, do_send, do_recv)
    dqkv_moves = Exchange(place, pairs, head_out, dqkv_in, dqkv_send, dqkv_recv)
    halves = (lower, upper)
    xs[lower, :] = x[kept, :]
    for half in range(2):
        if half:
            x_swap.wait()
            cot_swap = swap(1, cot_hbm.at[moved], og.at[upper])
        project_qkv(
            half, xs, gain1, shift1, wqkv, (bq, None, bv), head_out, lhs.at[0],
            (lambda part: None) if half else (lambda part: loads[part].wait()),
        )
        for pair in range(pairs):
            qkv_moves.start(pair, half, halves[half])

    core_moves = {}

    def to_core(name, src, dst):
        i = len(core_moves)
        core_moves[name] = rcopy(src, dst, core_send.at[i], core_recv.at[i], place.core())
        core_moves[name].start()

    waited = set()

    def from_core(*names):
        for name in names:
            if name not in waited:
                waited.add(name)
                core_moves[name].wait()

    to_core("n1", lhs.at[0], s_lhs.at[0])
    block_ones(place, keys, blocks)
    loads[5 + TILES].wait()
    fill_bias(place, picks, bias, blocks)

    for pair in range(pairs):
        for half in range(2):
            qkv_moves.arrived(pair, half, halves[half])
        attend_pair(pair, by_head, bias, keys, k_t, v_t, small_out, raw, mass)
        att_moves.start(pair)
    for copy in count_moves:
        copy.wait_send()
    for k in range(1, wins):
        slot = counts.at[lax.rem(place.w + wins - k, wins)]
        rcopy(slot, slot, count_send.at[k], count_recv.at[k], place.win_at(k)).wait_recv()
    sizes = counts[0]
    for k in range(1, wins):
        sizes = sizes + counts[k]
    first_row = lax.broadcasted_iota(jnp.int32, (8, 128), 0) == 0
    loads[3].wait()
    cot_swap.wait()
    own_size = jnp.sum(
        jnp.where(first_row & (lane == ids[place.window]), sizes, 0.0), keepdims=True
    )
    og[...] = (og[...].astype(f32) * (windows * wins / (GROUPS * own_size))).astype(bf16)
    to_core("og", og, s_og)
    out_grad = og[...]
    for t in range(TILES):
        loads[4 + t].wait()
    early = dact.shape[0] > 1
    if early:
        for t in range(TILES):
            dact[t] = mm_nt(out_grad, down_tile(t)[...])

    for pair in range(pairs):
        att_moves.arrived(pair)
    for h in range(HEADS):
        slot, pair = divmod(h, pairs)
        lhs[1, h * HEAD_DIM : (h + 1) * HEAD_DIM, :] = att_in[slot, pair]
    to_core("att", lhs.at[1], s_lhs.at[1])
    for copy in [loads[4 + TILES]] + loads[6 + TILES :]:
        copy.wait()


    def fill(index, cols, parts):
        @pl.loop(0, D // 256)
        def _(i):
            rows = span(i * 256, 256)
            (left, right), (left2, right2) = parts
            total = mm(left[rows, :], right) + mm(left2[rows, :], right2)
            out[index, rows, cols] = total.astype(bf16)

    def stream(p):
        if p < 8:
            i, h = (p % 4) // 2, p % 2
            index, other = (p // 4) * 4 + ours + i, (p // 4) * 4 + theirs + i
            col = other_col = h * HALF
            cols = slice(col, col + HALF)
            if p < 4:
                from_core("og", ("act", i))
                parts = ((act_t.at[ours + i], og[:, cols]), (s_act.at[i], s_og[:, cols]))
            else:
                from_core("n2", ("pg", i))
                parts = ((n2_t, pg[ours + i, :, cols]), (s_n2, s_pg[i, :, cols]))
        else:
            i = (3, 0, 1, 2)[p - 8]
            index = other = 8 + i
            col = pl.multiple_of(c * HALF, HALF)
            other_col = pl.multiple_of((1 - c) * HALF, HALF)
            cols = pl.ds(col, HALF)
            side = i // 3
            from_core(("n1", "att")[side], ("rhs", i))
            parts = ((lhs.at[side], rhs[i, :, cols]), (s_lhs.at[side], s_rhs[i]))
        fill(index, cols, parts)
        return reduce_piece(
            place, ORDERS[p], out, out_hbm, store.at[p],
            (index, col), (other, other_col),
            [ref.at[p] for ref in (r0, r1, r2, r3)],
            *(ref.at[p] for ref in (rl, piece_send, piece_recv, free)),
        )

    streams = {}
    ended = set()

    def go(p):
        if p not in streams:
            if p == VECTORS:
                streams[p] = reduce_vectors(place, vec_out, run, got, vec_send, vec_recv)
            else:
                streams[p] = stream(p)
        if p not in ended and next(streams[p], True) is not None:
            ended.add(p)


    hidden = xs[...].astype(f32) + (mm(lhs[1].T, wo[...]) + row(bo))
    vhat, rstd = normalise(hidden)
    n2 = (vhat * row(gain2) + row(shift2)).astype(bf16)
    n2_t[...] = n2.T
    to_core("n2", n2_t, s_n2)
    vec = run.at[0]
    vec[...] = jnp.zeros_like(vec)
    total = jnp.zeros(hidden.shape, f32)
    err = jnp.zeros(hidden.shape, f32)
    for i in range(TILES):
        t = (theirs if i < 2 else ours) + i % 2
        up_part, down_part = up_tile(t)[...], down_tile(t)[...]
        pre = mm(n2, up_part) + up_bias[pl.ds(t, 1), :]
        phi = 0.5 * (1.0 + lax.erf(pre * (0.5**0.5)))
        act = (pre * phi).astype(bf16)
        act_t[t] = act.T
        slope = phi + pre * (jnp.exp(-0.5 * pre * pre) * (1.0 / math.sqrt(2.0 * math.pi)))
        back = dact[t] if early else mm_nt(out_grad, down_part)
        grad = (back * slope).astype(bf16)
        pg[t] = grad
        if i < 2:
            to_core(("act", i), act_t.at[t], s_act.at[i])
            to_core(("pg", i), pg.at[t], s_pg.at[i])
        total = total + mm(act, down_part)
        err = err + mm_nt(grad, up_part)
        vec[pl.ds(8 + t, 1), :] = jnp.sum(grad.astype(f32), axis=0, keepdims=True)
        if i == 2:
            go(0)
            go(1)
    pl.semaphore_signal(core_free, inc=1, device_id=place.core(), device_id_type=MESH)
    place.core_free = core_free
    dv, dgain, dshift = norm_back(err, vhat, rstd, row(gain2))
    hidden_grad = out_grad.astype(f32) + dv
    branch = hidden_grad.astype(bf16)
    rhs[3] = branch
    datt_t = mm_nt(branch, wo[...]).astype(bf16).T
    for pair in range(pairs):
        att_moves.sent(pair)
    small_out[:HEADS] = datt_t.reshape(HEADS, HEAD_DIM, 2 * tokens)
    for pair in range(pairs):
        do_moves.start(pair)
    their_cols = pl.ds(pl.multiple_of((1 - c) * HALF, HALF), HALF)
    to_core(("rhs", 3), rhs.at[3, :, their_cols], s_rhs.at[3])
    hg[...] = hidden_grad
    result = (hidden + total + row(bdown)).astype(bf16)
    y[kept, :] = result[:tokens]
    y_sent[0] = result[tokens:]
    y_swap = swap(2, y_sent.at[0], y_got.at[0])
    vec[4:5, :] = jnp.sum(branch.astype(f32), axis=0, keepdims=True)
    vec[5:6, :] = dgain
    vec[6:7, :] = dshift
    vec[7:8, :] = jnp.sum(out_grad.astype(f32), axis=0, keepdims=True)
    for pair in range(pairs):
        for half in range(2):
            qkv_moves.sent(pair, half, halves[half])


    done_pairs = [0]

    def attention():
        pair = done_pairs[0]
        if pair == pairs:
            return
        done_pairs[0] += 1
        do_moves.arrived(pair)

        def scoped(dk, dv):
            attend_pair_back(
                pair, by_head, do_in, bias, raw, mass, keys, k_t, v_t, dk, dv, head_out
            )

        summed = pltpu.VMEM((HEAD_DIM, length), f32)
        pl.run_scoped(scoped, summed, summed)
        dqkv_moves.start(pair)

    def inputs():
        while done_pairs[0] < pairs:
            attention()
        for pair in range(pairs):
            dqkv_moves.arrived(pair)
        result = input_back(xs, gain1, dqkv_in, hg, wqkv, rhs, vec)
        for i in range(3):
            to_core(("rhs", i), rhs.at[i, :, their_cols], s_rhs.at[i])
        dx[kept, :] = result[:tokens]
        y_sent[1] = result[tokens:]
        swaps.append(swap(3, y_sent.at[1], y_got.at[1]))

    swaps = [y_swap]
    actions = {
        "A": attention,
        "W": inputs,
        "X": lambda: from_core(("rhs", 0), ("rhs", 1), ("rhs", 2)),
        "v": functools.partial(go, VECTORS),
    }
    for token in "".join(SCHEDULE):
        if token in actions:
            actions[token]()
        else:
            go(int(token, 16))
    everything = list(range(2 * OWN)) + [VECTORS]
    while len(ended) < len(everything):
        for p in everything:
            go(p)
    from_core(*core_moves)
    for copy in swaps:
        copy.wait()
    y[moved, :] = y_got[0]
    dx[moved, :] = y_got[1]
    for pair in range(pairs):
        do_moves.sent(pair)
        dqkv_moves.sent(pair)


def widen_kernel(
    sums, vec, y, dx, down, up, wq, wk, wv, wo, y_out, dx_out, *rest
):
    low, high, load, store = rest[-4:]
    half = D // 2
    loads = []
    for i in range(4 * OWN):
        rows = slice((i % 2) * half, (i % 2 + 1) * half)
        loads.append(pltpu.make_async_copy(sums.at[i // 2, rows], low.at[i], load.at[i]))
        loads[-1].start()
    y_out[...] = y[...].reshape(y_out.shape)
    dx_out[...] = dx[...].reshape(dx_out.shape)
    for r in range(8):
        rest[r][...] = vec[r, :]
    for r in range(TILES):
        rest[8][r * D : (r + 1) * D] = vec[8 + r, :]
    stores = []
    for i, copy in enumerate(loads):
        block, part = divmod(i, 2)
        rows = slice(part * half, (part + 1) * half)
        if block < 4:
            target = down.at[slice(block * D + part * half, block * D + (part + 1) * half)]
        elif block < 8:
            target = up.at[rows, slice((block - 4) * D, (block - 3) * D)]
        else:
            target = (wq, wk, wv, wo)[block - 8].at[rows]
        copy.wait()
        high[i] = low[i].astype(f32)
        stores.append(pltpu.make_async_copy(high.at[i], target, store.at[i]))
        stores[-1].start()
    for copy in stores:
        copy.wait()


def widen(sums, vec, y, dx, shape):
    struct = jax.ShapeDtypeStruct
    square = struct((D, D), f32)
    vectors = [struct((D,), f32)] * 8 + [struct((FF,), f32)]
    chunks = 4 * OWN
    return pl.pallas_call(
        widen_kernel,
        out_shape=[struct((FF, D), f32), struct((D, FF), f32)]
        + [square] * 4
        + [struct(shape, bf16)] * 2
        + vectors,
        in_specs=[anywhere, in_vmem, in_vmem, in_vmem],
        out_specs=[anywhere] * 6 + [in_vmem] * 11,
        scratch_shapes=[
            pltpu.VMEM((chunks, D // 2, D), bf16),
            pltpu.VMEM((chunks, D // 2, D), f32),
            pltpu.SemaphoreType.DMA((chunks,)),
            pltpu.SemaphoreType.DMA((chunks,)),
        ],
        compiler_params=pltpu.CompilerParams(vmem_limit_bytes=VMEM_LIMIT),
    )(sums, vec, y, dx)


def body(
    tokens,
    cotangent,
    group_ids,
    random_blocks,
    norm1_gain,
    norm1_bias,
    query_weight,
    query_bias,
    key_weight,
    value_weight,
    value_bias,
    out_weight,
    out_bias,
    norm2_gain,
    norm2_bias,
    up_weight,
    up_bias,
    down_weight,
    down_bias,
):
    seqs, wins = lax.axis_size("seq"), lax.axis_size("win")
    windows, here, _ = tokens.shape
    length = here * seqs
    blocks = length // BLOCK
    rows = windows * here
    group = seqs // 2
    pairs = -(-HEADS // group)
    slots = pairs * group
    layer_steps = (seqs // 8).bit_length() - 1
    extra = -(-(HEAD_DIM + 3 * blocks) // 128) * 128 - HEAD_DIM
    dims = (wins, seqs, windows, pairs)
    struct = jax.ShapeDtypeStruct
    dma = pltpu.SemaphoreType.DMA
    vmem = pltpu.VMEM

    x = tokens.reshape(rows, D)
    layer_slots = max(layer_steps, 1)
    pieces = 2 * OWN
    early = TILES if length <= 2048 else 1
    y, dx, vec_sums, sums = pl.pallas_call(
        functools.partial(layer_kernel, dims),
        out_shape=(
            struct((rows, D), bf16),
            struct((rows, D), bf16),
            struct((VEC_ROWS, D), f32),
            struct((pieces, D, D), bf16),
        ),
        in_specs=[in_smem] + [in_vmem] * 10 + [anywhere] * 8,
        out_specs=(in_vmem, in_vmem, in_vmem, anywhere),
        scratch_shapes=[
            pltpu.SMEM(random_blocks.shape, jnp.int32),
            vmem((pieces, D, D), bf16),
            vmem((rows, D), bf16),
            vmem((2, here, D), bf16),
            vmem((2, here, D), bf16),
            vmem((3, D, D), bf16),
            vmem((D, D), bf16),
            vmem((rows, D), bf16),
            vmem((2, D, rows), bf16),
            vmem((4, rows, D), bf16),
            vmem((D, rows), bf16),
            vmem((TILES, D, rows), bf16),
            vmem((TILES, rows, D), bf16),
            vmem((rows, D), f32),
            vmem((early, rows, D) if early > 1 else (1, 8, 128), f32),
            vmem((8, D), f32),
            vmem((rows, D), bf16),
            vmem((D, rows), bf16),
            vmem((2, D, rows), bf16),
            vmem((2, rows, D), bf16),
            vmem((2, D, rows), bf16),
            vmem((4, rows, HALF), bf16),
            vmem((slots, 3 * HEAD_DIM, rows), bf16),
            vmem((group, pairs, 3 * HEAD_DIM, rows), bf16),
            vmem((slots, HEAD_DIM, rows), bf16),
            vmem((group, pairs, HEAD_DIM, rows), bf16),
            vmem((group, pairs, HEAD_DIM, rows), bf16),
            vmem((group, pairs, 3 * HEAD_DIM, rows), bf16),
            vmem((extra, length), bf16),
            vmem((pairs, HEAD_DIM, length), f32),
            vmem((pairs, 1, length), f32),
            vmem((length, HEAD_DIM + extra), bf16),
            vmem((HEAD_DIM, length), bf16),
            vmem((HEAD_DIM, length), bf16),
            vmem((wins, 8, 128), f32),
            vmem((pieces, D // 2, HALF), bf16),
            vmem((pieces, D // 4, HALF), bf16),
            vmem((pieces, D // 8, HALF), bf16),
            vmem((pieces, D // 16, HALF), bf16),
            vmem((pieces, layer_slots, D // 16, HALF), bf16),
            vmem((5, VEC_ROWS, D), f32),
            vmem((7 + layer_slots, VEC_ROWS, D), f32),
            dma((6 + 2 * TILES,)),
            dma((pieces, 2)),
            dma((pieces, 9 + layer_slots)),
            dma((pieces, 9 + layer_slots)),
            pltpu.SemaphoreType.REGULAR((pieces, 4)),
            pltpu.SemaphoreType.REGULAR,
            dma((12,)),
            dma((12,)),
        ]
        + [dma((group, pairs, 2))] * 8
        + [dma((wins,))] * 2
        + [dma((6 + layer_slots,))] * 2
        + [dma((4,))] * 2,
        compiler_params=pltpu.CompilerParams(
            collective_id=0, has_side_effects=True, vmem_limit_bytes=VMEM_LIMIT
        ),
    )(
        group_ids, x, norm1_gain, norm1_bias, query_bias, value_bias, out_bias,
        norm2_gain, norm2_bias, up_bias, down_bias, random_blocks, cotangent.reshape(rows, D), query_weight,
        key_weight, value_weight, out_weight, up_weight, down_weight,
    )

    (
        down_grad, up_grad, query_grad, key_grad, value_grad, out_grad, output, input_grad,
        gain1_grad, shift1_grad, query_bias_grad, value_bias_grad, out_bias_grad,
        gain2_grad, shift2_grad, down_bias_grad, up_bias_grad,
    ) = widen(sums, vec_sums, y, dx, tokens.shape)
    return (
        output, input_grad, gain1_grad, shift1_grad, query_grad, query_bias_grad, key_grad,
        value_grad, value_bias_grad, out_grad, out_bias_grad, gain2_grad, shift2_grad, up_grad,
        up_bias_grad, down_grad, down_bias_grad,
    )


def solution(mesh):
    split = P("win", "seq", None)
    return jax.shard_map(
        body,
        mesh=mesh,
        in_specs=(split, split, P("win"), P("win", None, None)) + (P(),) * 15,
        out_specs=(split, split) + (P(),) * 15,
        check_vma=False,
    )
```

time: 1090 us -> 205 us (0.19); the launches traced: 1070 us -> 204 us
  waiting for transfers between devices: 416 us -> 0 us
  local copies, waits for them, and re-layouts: 330 us -> 1.37 us
  Pallas kernels: 0 us -> 202 us
  matrix products: 136 us -> 0 us
  other arithmetic: 82.3 us -> 0 us
  blocking collectives: 51.3 us -> 0 us
  starting transfers between devices: 41.6 us -> 0 us
  between operations: 16 us -> 0.84 us
    psum x3 -> x0, waiting for transfers between devices: 405 us -> none  [the longest x1 363 us: body(): lax.psum((gain1_total, shift1_total, query_total, query_bias_total, key_t...]
    pallas_call x0 -> x2, Pallas kernels: none -> 202 us  [the longest x1 186 us: body(): pl.pallas_call(functools.partial(layer_kernel, dims), out_shape=(struct((...]
    dot_general x56 -> x0, matrix products: 136 us -> none  [the longest x12 39.7 us: weight_grad(): jnp.einsum('wld,wle->de', inputs, gradient, preferred_element_type=jnp.fl...]
    unnamed x311 -> x1, local copies, waits for them, and re-layouts: 94.7 us -> 1.37 us
    another operation x29 -> x0, local copies, waits for them, and re-layouts: 67.3 us -> none
    concatenate x4 -> x0, local copies, waits for them, and re-layouts: 61.8 us -> none  [the longest x2 59.8 us: build_context(): return jnp.concatenate([sliding, global_pair, random_part], axis=2)]
    psum x2 -> x0, blocking collectives: 51.3 us -> none  [the longest x1 40.8 us: body(): lax.psum((gain1_total, shift1_total, query_total, query_bias_total, key_t...]
    reshape x14 -> x0, local copies, waits for them, and re-layouts: 45.5 us -> none  [the longest x2 11.3 us: body(): value_grad.reshape(WIN_MB, BLK_DEV, key_slots, BLOCK, D)]
  transfers between devices with their start and end apart: 15 -> 0, of which waited for: 4 -> 0; matrix products, arithmetic and copies ran while one was open for 19% -> 0% of each run, Pallas kernels for 0% -> 0%
where the time goes in v3:
time: 205 us; the launch traced here: 204 us
  Pallas kernels  202 us (99%)
    pallas_call x1, Pallas kernels, body(): pl.pallas_call(functools.partial(layer_kernel, dims), out_shape=(struct((...  186 us
    pallas_call x1, Pallas kernels, widen(): pl.pallas_call(widen_kernel, out_shape=[struct((FF, D), f32), struct((D,...  15.9 us

profile of v3, /device:TPU:0, one launch (start us, length us, event | category | flops | bytes accessed | tf_op | source)
XLA Modules:
  0.0 204.4 jit_solution(18030615290224205265)
XLA Ops:
  0.7 1.4 copy.36.picks_hbm
  2.0 186.3 %shard_map.314 = (bf16[256,768]{1,0:T(8,128)(2,1)}, bf16[256,768]{1,0:T(8,128)(2,1)}, f32[16,768]{1,0:T(8,128)}, bf16[12,768,768]{2,1,0:T(8,128)(2,1)}) custom-call(s32[2]{0:T(128)} %ids.1, bf16[256,768]{1,0:T(8,128)(2,1)} %bitcast.2, f32[768]{0:T(1024)} %gain1.1, f32[768]{0:T(1024)} %shift1.1, f32[768]{0:T(1024)} %bq.1, f32[768]{0:T(1024)} %bv.1, f32[768]{0:T(1024)} %bo.1, ...), custom_call_target="tpu_custom_call" | custom-call | tf_op jit(solution)/shard_map/pallas_call | solution.py:874
  188.3 15.9 %shard_map.315 = (f32[3072,768]{1,0:T(8,128)}, f32[768,3072]{1,0:T(8,128)}, f32[768,768]{1,0:T(8,128)}, f32[768,768]{1,0:T(8,128)}, f32[768,768]{1,0:T(8,128)}, ...) custom-call(bf16[12,768,768]{2,1,0:T(8,128)(2,1)} %get-tuple-element, ...), custom_call_target="tpu_custom_call" | custom-call | tf_op jit(solution)/shard_map/pallas_call | solution.py:816

commit v4 on v3

--- a/solution.py
+++ b/solution.py
@@ -22,14 +22,14 @@
 VECTORS = 12
 ORDERS = (
     "labh", "balh", "ablh", "balh",
-    "ablh", "balh", "ablh", "blah",
+    "ablh", "balh", "ablh", "balh",
     "ablh", "balh", "ablh", "balh",
 )
 SCHEDULE = (
-    "2301AAA23504123765Wv01234vX9876v45ab0v79",
-    "184v25630v1a647vb215983026b49a71853260b4",
-    "93a178541162722530b963a380047b4594a8655b",
-    "a9676b877a898899abaabb",
+    "2014AAA25403216057Wv36124v0X875v936b8v1a",
+    "932v67405vb71a3v82109684a2b59713426a08b5",
+    "97132641a526308b90754a8b594a36b8376a9b77",
+    "8989abab",
 )
 
 MESH = pl.DeviceIdType.MESH
@@ -158,8 +158,8 @@
         return rcopy(
             self.out.at[target * self.pairs + pair, :, lanes],
             self.into.at[place.g, pair, :, lanes],
-            self.send.at[k, pair, part],
-            self.recv.at[k, pair, part],
+            self.send.at[pair, part],
+            self.recv.at[pair, part],
             place.group_at(k),
         )
 
@@ -172,24 +172,18 @@
         lax.fori_loop(1, place.size, one, 0)
         self.into[place.g, pair, :, lanes] = self.out[place.g * self.pairs + pair, :, lanes]
 
+    def whole(self, ref, pair, part, lanes):
+        return rcopy(
+            ref, ref, self.send.at[pair, part], self.recv.at[pair, part], self.place.group_at(1)
+        )
+
     def arrived(self, pair, part=0, lanes=slice(None)):
-        def one(k, carry):
-            place = self.place
-            slot = self.into.at[lax.rem(place.g + place.size - k, place.size), pair, :, lanes]
-            rcopy(
-                slot, slot, self.send.at[k, pair, part], self.recv.at[k, pair, part],
-                place.group_at(k),
-            ).wait_recv()
-            return carry
-
-        lax.fori_loop(1, self.place.size, one, 0)
+        held = self.into.at[pl.ds(0, self.place.size - 1), pair, :, lanes]
+        self.whole(held, pair, part, lanes).wait_recv()
 
     def sent(self, pair, part=0, lanes=slice(None)):
-        def one(k, carry):
-            self.copy(k, pair, part, lanes).wait_send()
-            return carry
-
-        lax.fori_loop(1, self.place.size, one, 0)
+        held = self.out.at[pl.ds(0, self.place.size - 1), :, lanes]
+        self.whole(held, pair, part, lanes).wait_send()
 
 
 Q_ROWS, K_ROWS, V_ROWS = (slice(i * HEAD_DIM, (i + 1) * HEAD_DIM) for i in range(3))
@@ -348,7 +342,7 @@
         first = (window * place.size + group // 2) * 2
         for side in range(2):
             for r in range(RAND):
-                pick = picks[place.window, first + side, r]
+                pick = picks[r, place.window, first + side]
                 count = count + jnp.where((key == pick) & (query == first + side), 1.0, 0.0)
         listed = count > 0.0
         rest = jnp.where(listed, jnp.log(jnp.maximum(count, 1.0)), masked_score)
@@ -403,7 +397,7 @@
         if i:
             source = bufs[i - 1]
             at(away, size)[...] = at(away, size)[...] + source[span((1 - bit) * size, size)]
-        cp = rcopy(at(away, size), bufs[i], send.at[i], recv.at[i], partner)
+        cp = rcopy(at(away, size), bufs[i], send, recv.at[i], partner)
         cp.start()
         if i:
             at(keep, size)[...] = at(keep, size)[...] + source[span(bit * size, size)]
@@ -411,35 +405,30 @@
         spans.append((keep, size))
         yield
         cp.wait()
-        pl.semaphore_signal(free.at[i], inc=1, device_id=partner, device_id_type=MESH)
+        pl.semaphore_signal(free, inc=1, device_id=partner, device_id_type=MESH)
     held = at(start, size)
     held[...] = held[...] + bufs[-1][...]
     for i in range(place.layer_steps):
-        cp = rcopy(held, rl.at[i], send.at[9 + i], recv.at[9 + i], place.layer_swap(i))
+        cp = rcopy(held, rl.at[i], send, recv.at[9 + i], place.layer_swap(i))
         cp.start()
         cp.wait()
         held[...] = held[...] + rl[i]
+    pl.semaphore_wait(free, len(hops))
     for i in reversed(range(len(hops))):
-        pl.semaphore_wait(free.at[i], 1)
         held = at(*spans[i])
-        cp = rcopy(held, held, send.at[4 + i], recv.at[4 + i], hops[i][1])
+        cp = rcopy(held, held, send, recv.at[4 + i], hops[i][1])
         cp.start()
         yield
         cp.wait()
     place.core_open()
     held = buf.at[:, cols]
-    cp = rcopy(held, held, send.at[8], recv.at[8], place.core())
+    cp = rcopy(held, held, send, recv.at[8], place.core())
     cp.start()
     yield
     cp.wait()
-    copies = []
-    for i, (block, column) in enumerate((mine, other)):
+    for block, column in (mine, other):
         where = (block, slice(None), pl.ds(column, HALF))
-        copies.append(pltpu.make_async_copy(out.at[where], out_hbm.at[where], store.at[i]))
-        copies[-1].start()
-    yield
-    for copy in copies:
-        copy.wait()
+        pltpu.make_async_copy(out.at[where], out_hbm.at[where], store).start()
 
 
 def reduce_vectors(place, out, run, got, send, recv):
@@ -642,7 +631,7 @@
             parts = ((lhs.at[side], rhs[i, :, cols]), (s_lhs.at[side], s_rhs[i]))
         fill(index, cols, parts)
         return reduce_piece(
-            place, ORDERS[p], out, out_hbm, store.at[p],
+            place, ORDERS[p], out, out_hbm, store,
             (index, col), (other, other_col),
             [ref.at[p] for ref in (r0, r1, r2, r3)],
             *(ref.at[p] for ref in (rl, piece_send, piece_recv, free)),
@@ -688,8 +677,8 @@
         err = err + mm_nt(grad, up_part)
         vec[pl.ds(8 + t, 1), :] = jnp.sum(grad.astype(f32), axis=0, keepdims=True)
         if i == 2:
-            go(0)
-            go(1)
+            for p in (0, 1, 4, 5):
+                go(p)
     pl.semaphore_signal(core_free, inc=1, device_id=place.core(), device_id_type=MESH)
     place.core_free = core_free
     dv, dgain, dshift = norm_back(err, vhat, rstd, row(gain2))
@@ -764,6 +753,7 @@
     while len(ended) < len(everything):
         for p in everything:
             go(p)
+    pltpu.make_async_copy(out, out_hbm, store).wait()
     from_core(*core_moves)
     for copy in swaps:
         copy.wait()
@@ -882,7 +872,7 @@
         in_specs=[in_smem] + [in_vmem] * 10 + [anywhere] * 8,
         out_specs=(in_vmem, in_vmem, in_vmem, anywhere),
         scratch_shapes=[
-            pltpu.SMEM(random_blocks.shape, jnp.int32),
+            pltpu.SMEM((RAND, windows, blocks), jnp.int32),
             vmem((pieces, D, D), bf16),
             vmem((rows, D), bf16),
             vmem((2, here, D), bf16),
@@ -925,24 +915,25 @@
             vmem((5, VEC_ROWS, D), f32),
             vmem((7 + layer_slots, VEC_ROWS, D), f32),
             dma((6 + 2 * TILES,)),
-            dma((pieces, 2)),
-            dma((pieces, 9 + layer_slots)),
-            dma((pieces, 9 + layer_slots)),
-            pltpu.SemaphoreType.REGULAR((pieces, 4)),
+            dma,
+            dma((pieces,)),
+            dma((pieces, 9 + layer_steps)),
+            pltpu.SemaphoreType.REGULAR((pieces,)),
             pltpu.SemaphoreType.REGULAR,
             dma((12,)),
             dma((12,)),
         ]
-        + [dma((group, pairs, 2))] * 8
+        + [dma((pairs, 2))] * 2
+        + [dma((pairs, 1))] * 6
         + [dma((wins,))] * 2
-        + [dma((6 + layer_slots,))] * 2
+        + [dma((6 + layer_steps,))] * 2
         + [dma((4,))] * 2,
         compiler_params=pltpu.CompilerParams(
             collective_id=0, has_side_effects=True, vmem_limit_bytes=VMEM_LIMIT
         ),
     )(
         group_ids, x, norm1_gain, norm1_bias, query_bias, value_bias, out_bias,
-        norm2_gain, norm2_bias, up_bias, down_bias, random_blocks, cotangent.reshape(rows, D), query_weight,
+        norm2_gain, norm2_bias, up_bias, down_bias, jnp.transpose(random_blocks, (2, 0, 1)), cotangent.reshape(rows, D), query_weight,
         key_weight, value_weight, out_weight, up_weight, down_weight,
     )
 

time: 205 us -> 198 us (0.966)
  Pallas kernels: 202 us -> 197 us
    pallas_call x1, Pallas kernels: 186 us -> 181 us  [body(): pl.pallas_call(functools.partial(layer_kernel, dims), out_shape=(struct((...]
where the time goes in v4:
time: 198 us
  Pallas kernels  197 us (99%)
    pallas_call x1, Pallas kernels, body(): pl.pallas_call(functools.partial(layer_kernel, dims), out_shape=(struct((...  181 us
    pallas_call x1, Pallas kernels, widen(): pl.pallas_call(widen_kernel, out_shape=[struct((FF, D), f32), struct((D,...  15.9 us

profile of v4, /device:TPU:0, one launch (start us, length us, event | category | flops | bytes accessed | tf_op | source)
XLA Modules:
  0.0 198.1 jit_solution(11832334066830993611)
XLA Ops:
  0.7 181.3 %shard_map.314 = (bf16[256,768]{1,0:T(8,128)(2,1)}, bf16[256,768]{1,0:T(8,128)(2,1)}, f32[16,768]{1,0:T(8,128)}, bf16[12,768,768]{2,1,0:T(8,128)(2,1)}) custom-call(s32[2]{0:T(128)} %ids.1, bf16[256,768]{1,0:T(8,128)(2,1)} %bitcast.3, f32[768]{0:T(1024)} %gain1.1, f32[768]{0:T(1024)} %shift1.1, f32[768]{0:T(1024)} %bq.1, f32[768]{0:T(1024)} %bv.1, f32[768]{0:T(1024)} %bo.1, ...), custom_call_target="tpu_custom_call" | custom-call | tf_op jit(solution)/shard_map/pallas_call | solution.py:864
  182.0 15.9 %shard_map.315 = (f32[3072,768]{1,0:T(8,128)}, f32[768,3072]{1,0:T(8,128)}, f32[768,768]{1,0:T(8,128)}, f32[768,768]{1,0:T(8,128)}, f32[768,768]{1,0:T(8,128)}, ...) custom-call(bf16[12,768,768]{2,1,0:T(8,128)(2,1)} %get-tuple-element, ...), custom_call_target="tpu_custom_call" | custom-call | tf_op jit(solution)/shard_map/pallas_call | solution.py:806

commit v5 on v4

--- a/solution.py
+++ b/solution.py
@@ -532,6 +532,9 @@
     xs[lower, :] = x[kept, :]
     for half in range(2):
         if half:
+            block_ones(place, keys, blocks)
+            loads[5 + TILES].wait()
+            fill_bias(place, picks, bias, blocks)
             x_swap.wait()
             cot_swap = swap(1, cot_hbm.at[moved], og.at[upper])
         project_qkv(
@@ -557,9 +560,6 @@
                 core_moves[name].wait()
 
     to_core("n1", lhs.at[0], s_lhs.at[0])
-    block_ones(place, keys, blocks)
-    loads[5 + TILES].wait()
-    fill_bias(place, picks, bias, blocks)
 
     for pair in range(pairs):
         for half in range(2):

time: 198 us -> 198 us (level)
  no operation moved by 1% of the time
where the time goes in v5:
time: 198 us
  Pallas kernels  197 us (99%)
    pallas_call x1, Pallas kernels, body(): pl.pallas_call(functools.partial(layer_kernel, dims), out_shape=(struct((...  181 us
    pallas_call x1, Pallas kernels, widen(): pl.pallas_call(widen_kernel, out_shape=[struct((FF, D), f32), struct((D,...  15.9 us

profile of v5, /device:TPU:0, one launch (start us, length us, event | category | flops | bytes accessed | tf_op | source)
XLA Modules:
  0.0 198.2 jit_solution(16491526624405202487)
XLA Ops:
  0.7 181.4 %shard_map.314 = (bf16[256,768]{1,0:T(8,128)(2,1)}, bf16[256,768]{1,0:T(8,128)(2,1)}, f32[16,768]{1,0:T(8,128)}, bf16[12,768,768]{2,1,0:T(8,128)(2,1)}) custom-call(s32[2]{0:T(128)} %ids.1, bf16[256,768]{1,0:T(8,128)(2,1)} %bitcast.3, f32[768]{0:T(1024)} %gain1.1, f32[768]{0:T(1024)} %shift1.1, f32[768]{0:T(1024)} %bq.1, f32[768]{0:T(1024)} %bv.1, f32[768]{0:T(1024)} %bo.1, ...), custom_call_target="tpu_custom_call" | custom-call | tf_op jit(solution)/shard_map/pallas_call | solution.py:864
  182.1 15.9 %shard_map.315 = (f32[3072,768]{1,0:T(8,128)}, f32[768,3072]{1,0:T(8,128)}, f32[768,768]{1,0:T(8,128)}, f32[768,768]{1,0:T(8,128)}, f32[768,768]{1,0:T(8,128)}, ...) custom-call(bf16[12,768,768]{2,1,0:T(8,128)(2,1)} %get-tuple-element, ...), custom_call_target="tpu_custom_call" | custom-call | tf_op jit(solution)/shard_map/pallas_call | solution.py:806
